TPU v7x, 256 devices: a whole 4x4x8 slice. The times are simulated.
256 devices in a mesh: row: 64 (over x, y_lo, z), panel: 4 (over y_hi, core).
Axes of the slice: x: 4, y: 4 (y_hi: 2, y_lo: 2; y = y_hi * 2 + y_lo), z: 8, core: 2. Of those that a mesh axis runs over, the one named last changes fastest.
Arguments:
- pixel_ids: int32 [65536], P('row'), may hold values from 0 to 65535, each once
- quad_offsets: int32 [2, 16, 65536], P(None, None, 'row'), may hold values from 0 to 7
- prior_factor: float32 [65536, 2048], P('row', 'panel'), may hold values from -0.036 to 0.036, as said below
Outputs:
- panel_factor: float32 [65536, 1024], P(('row', 'panel'))
Inputs may be any that keep to these rules, and one draw needn't show every extreme that they name: `pixel_ids`: each pixel of the grid appears in exactly one row. `prior_factor`: schur[panel_index] is positive definite.
All inputs are finite; a program needn't handle non-finite values.
Results may differ from a plain program's by a relative error of at most 0.0003.
Values sent between devices are 32-bit elements; how exact they have to be, the bound alone decides.
A program may use at most 128 MiB of HBM per device.

v0:
```python
import jax
import jax.numpy as jnp
from jax import lax
from jax.sharding import PartitionSpec as P

B = 1024


range_inverse = 1.0


def from_behind(block, axis, distance):
    devices = range(lax.axis_size(axis))
    route = [((i - distance) % len(devices), i) for i in devices]
    return lax.ppermute(block, axis, route)


def locate(pixel_ids, quad_offsets):
    column = (pixel_ids % 256).astype(jnp.float32)
    lines = (pixel_ids // 256).astype(jnp.float32)
    east = column[None, :] + (quad_offsets[0].astype(jnp.float32) + 0.5) / 8.0
    north = lines[None, :] + (quad_offsets[1].astype(jnp.float32) + 0.5) / 8.0
    return (east, north)


def cover_tile(east_rows, north_rows, east_cols, north_cols):
    count = east_rows.shape[0]

    def accumulate(index, running):
        east_one = lax.dynamic_index_in_dim(east_rows, index, 0, keepdims=False)
        north_one = lax.dynamic_index_in_dim(north_rows, index, 0, keepdims=False)
        apart_east = east_cols[:, :, None] - east_one[None, None, :]
        apart_north = north_cols[:, :, None] - north_one[None, None, :]
        return running + jnp.sum(
            jnp.exp(-(apart_east * apart_east + apart_north * apart_north) * range_inverse), axis=0
        )

    start = jnp.zeros((east_cols.shape[1], east_rows.shape[1]), jnp.float32)
    total = lax.fori_loop(0, count, accumulate, start)
    return total.T / float(count * count)


def local(pixel_ids, quad_offsets, prior_factor):
    panel_count = lax.axis_size("panel")
    row_count = lax.axis_size("row")
    block_rows = pixel_ids.shape[0]
    quarter_rows = block_rows // panel_count
    per_device = B // (row_count * panel_count)
    span_cols = panel_count * per_device
    row_pos = lax.axis_index("row")
    panel_pos = lax.axis_index("panel")
    east, north = locate(pixel_ids, quad_offsets)
    all_points = jnp.stack([east, north])
    own_points = lax.dynamic_slice_in_dim(all_points, panel_pos * quarter_rows, quarter_rows, 2)
    own_east = own_points[0]
    own_north = own_points[1]
    local_points = all_points.reshape(2, east.shape[0], panel_count, quarter_rows)[
        :, :, :, :per_device
    ]
    local_points = local_points.reshape(2, east.shape[0], span_cols)
    start_cols = jnp.zeros((quarter_rows, B), jnp.float32)

    def place(columns, held, source):
        tile = cover_tile(own_east, own_north, held[0], held[1])
        return lax.dynamic_update_slice(columns, tile, (jnp.int32(0), source * span_cols))

    def turn(index, carry):
        held, columns = carry
        columns = place(columns, held, (row_pos - index) % row_count)
        held = from_behind(held, "row", 1)
        return (held, columns)

    held, columns = lax.fori_loop(0, row_count - 1, turn, (local_points, start_cols))
    columns = place(columns, held, (row_pos - (row_count - 1)) % row_count)
    device_pos = row_pos * panel_count + panel_pos
    row_ids = jnp.arange(quarter_rows, dtype=jnp.int32)[:, None]
    col_ids = jnp.arange(B, dtype=jnp.int32)[None, :]
    on_diagonal = (row_ids < per_device) & (col_ids == device_pos * per_device + row_ids)
    cover = columns + jnp.where(on_diagonal, 1.0, 0.0).astype(jnp.float32)
    whole_rows = lax.all_to_all(prior_factor, "panel", split_axis=0, concat_axis=1, tiled=True)
    panel_prior = lax.all_gather(whole_rows[:per_device], ("row", "panel"), axis=0, tiled=True)
    update = jnp.dot(
        whole_rows,
        panel_prior.T,
        precision=lax.Precision.HIGHEST,
        preferred_element_type=jnp.float32,
    )
    schur = cover - update
    diag_rows = lax.all_gather(schur[:per_device], ("row", "panel"), axis=0, tiled=True)
    diag_factor = jnp.linalg.cholesky(diag_rows)
    return lax.linalg.triangular_solve(
        diag_factor, schur, left_side=False, lower=True, transpose_a=True
    )


def solution(mesh):
    return jax.shard_map(
        local,
        mesh=mesh,
        in_specs=(P("row"), P(None, None, "row"), P("row", "panel")),
        out_specs=P(("row", "panel"), None),
        check_vma=False,
    )
```

profile of v0, /device:TPU:1, one launch (start us, length us, event | category | flops | bytes accessed | tf_op | source)
XLA Modules:
  0.0 1338.5 jit_solution(4955843680710674743)
XLA Ops:
  6.5 6.9 all-to-all-start
  13.8 26.0 %all-to-all-done = f32[4,256,512]{2,1,0:T(8,128)S(1)} async-done(((f32[4,256,512]{2,1,0:T(8,128)}), f32[4,256,512]{2,1,0:T(8,128)S(1)}, u32[]{:S(2)}, u32[]{:S(2)}) %all-to-all-start) | async-done | bytes 2097184 | tf_op jit(solution)/shard_map/all_to_all | solution.py:80
  40.6 431.7 %while.68 = (s32[]{:T(128)}, f32[2,16,16]{2,1,0:T(8,128)S(1)}, f32[256,1024]{0,1:T(8,128)S(1)}, f32[16,256]{1,0:T(8,128)S(1)}, f32[16,256]{1,0:T(8,128)S(1)}, /*...) while((s32[]{:T(128)}, f32[2,16,16]{2,1,0:T(8,128)S(1)}, ...), condition=%wide.region_4.5_spmd, body=%wide.region_0.4_spmd.sunk | while | flops 466965 | bytes 123403 | solution.py:73
  44.7 4.1 collective-permute-done
  52.2 3.5 collective-permute-done
  59.0 3.5 collective-permute-done
  65.8 3.5 collective-permute-done
  72.6 3.5 collective-permute-done
  79.4 3.5 collective-permute-done
  86.2 3.9 collective-permute-done
  100.3 3.5 collective-permute-done
  107.1 3.5 collective-permute-done
  113.9 3.5 collective-permute-done
  120.7 3.5 collective-permute-done
  127.5 3.5 collective-permute-done
  134.4 3.6 collective-permute-done
  141.2 3.5 collective-permute-done
  182.1 3.6 collective-permute-done
  229.9 3.6 collective-permute-done
  277.6 3.6 collective-permute-done
  325.4 3.6 collective-permute-done
  373.2 3.6 collective-permute-done
  420.9 3.6 collective-permute-done
  468.7 3.6 collective-permute-done
  481.5 10.2 reshape.138
  491.6 16.1 %convolution_subtract_fusion = f32[256,1024]{1,0:T(8,128)S(1)} fusion(f32[256,2048]{0,1:T(8,128)S(1)} %bitcast.152, f32[1024,2048]{1,0:T(8,128)} %reshape.138, f32[256,1024]{1,0:T(8,128)S(1)} %dynamic_update_slice.13, s32[256]{0:T(256)S(1)} %iota_add_fusion, pred[256]{0:T(512)(128)(4,1)S(1)} %iota_compare_fusion.4), kind=kOutput, calls=%fused_computation.15 | convolution fusion | flops 6443761664 | bytes 12584192 | tf_op jit(solution)/shard_map/dot_general | solution.py:82
  509.3 476.6 %all-gather.7.cloned.1.call-done = f32[256,4,1024]{2,1,0:T(4,128)} async-done(((f32[1,4,1024]{2,1,0:T(4,128)}), f32[256,4,1024]{2,1,0:T(4,128)}) %all-gather.7.cloned.1.call-update) | async-done | bytes 4194320 | tf_op jit(solution)/shard_map/all_gather | solution.py:89
  985.9 5.3 reshape.140
  991.2 5.8 copy.69
  997.0 4.4 fusion
  1003.4 11.7 cholesky.223
  1017.6 9.8 custom-call.62
  1031.4 11.9 cholesky.244
  1043.9 9.8 custom-call.63
  1057.1 11.7 cholesky.468
  1069.4 9.8 custom-call.64
  1082.7 11.9 cholesky.487
  1095.3 9.8 custom-call.65
  1108.5 11.7 cholesky.506
  1120.9 10.2 custom-call.66
  1134.4 11.7 cholesky.526
  1146.8 9.8 custom-call.67
  1159.6 11.7 cholesky.546
  1171.9 9.8 custom-call.68
  1184.4 11.7 cholesky.564
  1207.1 4.9 select_select_fusion
  1211.9 22.8 %while.69 = (s32[]{:T(128)}, f32[1024,1024]{1,0:T(8,128)}, s32[8,2]{0,1:T(2,128)S(1)}, f32[8,128,128]{2,1,0:T(8,128)S(1)}, s32[]{:T(128)}) while((s32[]{:T(128)}, f32[1024,1024]{1,0:T(8,128)}, s32[8,2]{0,1:T(2,128)S(1)}, f32[8,128,128]{2,1,0:T(8,128)S(1)}, s32[]{:T(128)}) %tuple.176), condition=%wide.while_cond, body=%wide.while_body.sunk | while | flops 2 | bytes 131189 | solution.py:91
  1234.8 78.8 %custom-call.69 = f32[8,128,128]{1,2,0:T(8,128)S(1)} custom-call(f32[8,128,128]{2,1,0:T(8,128)S(1)} %get-tuple-element.405), custom_call_target="InvertDiagBlocksLowerTriangular" | custom-call | tf_op jit(solution)/shard_map/triangular_solve | solution.py:91
  (3613 shorter events, 608.9 us)
Async XLA Ops:
  6.5 33.3 %all-to-all-start = ((f32[4,256,512]{2,1,0:T(8,128)}), f32[4,256,512]{2,1,0:T(8,128)S(1)}, u32[]{:S(2)}, u32[]{:S(2)}) async-start(f32[4,256,512]{2,1,0:T(8,128)} %bitcast.153), calls=%async_computation | async-start | bytes 4194304 | tf_op jit(solution)/shard_map/all_to_all | solution.py:80
  13.5 468.0 %all-gather.5.cloned.1.call-start = ((), (), s32[]{:S(2)}) async-start(), calls=%async_computation.1 | async-start | bytes 8421376 | tf_op jit(solution)/shard_map/all_gather | solution.py:81
  40.5 945.5 %all-gather.7.cloned.1.call-start = ((), (), s32[]{:S(2)}) async-start(), calls=%async_computation.2 | async-start | bytes 4210688 | tf_op jit(solution)/shard_map/all_gather | solution.py:89
  40.6 8.3 collective-permute-start
  48.9 6.8 collective-permute-start
  55.7 6.8 collective-permute-start
  62.5 6.8 collective-permute-start
  69.3 6.8 collective-permute-start
  76.1 6.8 collective-permute-start
  82.9 7.2 collective-permute-start
  90.2 6.8 collective-permute-start
  97.0 6.8 collective-permute-start
  103.8 6.8 collective-permute-start
  110.6 6.8 collective-permute-start
  117.4 6.8 collective-permute-start
  124.2 6.8 collective-permute-start
  131.0 6.9 collective-permute-start
  137.9 6.8 collective-permute-start
  144.7 6.8 collective-permute-start
  151.6 6.8 collective-permute-start
  158.4 6.8 collective-permute-start
  165.2 6.8 collective-permute-start
  172.0 6.8 collective-permute-start
  178.8 6.9 collective-permute-start
  185.7 6.8 collective-permute-start
  192.5 6.8 collective-permute-start
  199.3 6.8 collective-permute-start
  206.1 6.8 collective-permute-start
  212.9 6.8 collective-permute-start
  219.8 6.8 collective-permute-start
  226.6 6.9 collective-permute-start
  233.5 6.8 collective-permute-start
  240.3 6.8 collective-permute-start
  247.1 6.8 collective-permute-start
  253.9 6.8 collective-permute-start
  260.7 6.8 collective-permute-start
  267.5 6.8 collective-permute-start
  274.3 6.9 collective-permute-start
  281.2 6.8 collective-permute-start
  288.0 6.8 collective-permute-start
  294.9 6.8 collective-permute-start
  301.7 6.8 collective-permute-start
  308.5 6.8 collective-permute-start
  315.3 6.8 collective-permute-start
  322.1 6.9 collective-permute-start
  369.9 6.9 collective-permute-start
  417.6 6.9 collective-permute-start
  465.4 6.9 collective-permute-start
  (25 other events, 257.1 us)
Sparse Core Ops, SparseCore 0:
  40.6 419.1 all-gather.4
  509.4 476.4 all-gather.6
where the time goes:
time: 1350 us; the launch traced here: 1340 us
  waiting for transfers between devices  725 us (54%)
  other arithmetic  416 us (31%)
  local copies, waits for them, and re-layouts  69 us (5%)
  matrix products  55.5 us (4%)
  loops' own time  45.8 us (3%)
  between operations  19.1 us (1%)
    all_gather x1, waiting for transfers between devices, local(): lax.all_gather(schur[:per_device], ('row', 'panel'), axis=0, tiled=True)  477 us
    ppermute x63, waiting for transfers between devices, from_behind(): return lax.ppermute(block, axis, route)  222 us
    another operation x31, other arithmetic, local(): diag_factor = jnp.linalg.cholesky(diag_rows)  173 us
    reduce_sum x1024, other arithmetic, accumulate(): jnp.sum(jnp.exp(-(apart_east * apart_east + apart_north * apart_north) *...  148 us
    another operation x3, other arithmetic, local(): lax.linalg.triangular_solve(diag_factor, schur, left_side=False, lower=Tr...  83.7 us
    another operation x64, loops' own time, cover_tile(): total = lax.fori_loop(0, count, accumulate, start)  42.9 us
  transfers between devices with their start and end apart: 66, of which 65 were waited for; matrix products, arithmetic and copies ran while one was open for 13% of the time, Pallas kernels for 0%

commit v1 on v0

v1 whole, which is shorter than its diff:
```python
import functools
import math

import jax
import jax.numpy as jnp
from jax import lax
from jax.experimental import pallas as pl
from jax.experimental.pallas import tpu as pltpu
from jax.sharding import PartitionSpec as P

f32, bf16 = jnp.float32, jnp.bfloat16
MESH = pl.DeviceIdType.MESH
NT = (((1,), (1,)), ((), ()))
B = 1024
Q = 16
VMEM_LIMIT = 56 * 2**20
SCALE = -math.log2(math.e) / 64.0


def place():
    row, panel = lax.axis_index("row"), lax.axis_index("panel")
    z = lax.rem(row, 8)
    y = panel // 2 * 2 + lax.rem(row // 8, 2)
    return row // 16, y, z, lax.rem(panel, 2)


def device(x, y, z, core):
    return {"row": (x * 2 + lax.rem(y, 2)) * 8 + z, "panel": y // 2 * 2 + core}


def meet(partners):
    barrier = pltpu.get_barrier_semaphore()
    for partner in partners:
        pl.semaphore_signal(barrier, inc=1, device_id=partner, device_id_type=MESH)
    pl.semaphore_wait(barrier, len(partners))


def send(src, dst, send_sem, recv_sem, target):
    return pltpu.make_async_remote_copy(
        src_ref=src, dst_ref=dst, send_sem=send_sem, recv_sem=recv_sem,
        device_id=target, device_id_type=MESH,
    )


def points_kernel(own, every, here, sz, rz, sb, rb):
    row, panel = lax.axis_index("row"), lax.axis_index("panel")
    z, base = lax.rem(row, 8), row // 8
    along = [{"row": base * 8 + lax.rem(z + d, 8), "panel": panel} for d in range(1, 8)]
    across = [{"row": lax.rem(base + d, 8) * 8 + z, "panel": panel} for d in range(1, 8)]
    meet(along + across)
    local = pltpu.make_async_copy(own, every.at[row], here)
    local.start()
    first = [send(own, every.at[row], sz.at[d], rz.at[d], along[d]) for d in range(7)]
    for copy in first:
        copy.start()
    local.wait()
    for copy in first:
        copy.wait_recv()
    slab = every.at[pl.ds(base * 8, 8)]
    second = [send(slab, slab, sb.at[d], rb.at[d], across[d]) for d in range(7)]
    for copy in second:
        copy.start()
    for copy in second:
        copy.wait_recv()
    for copy in first + second:
        copy.wait_send()


def gather_points(own):
    return pl.pallas_call(
        points_kernel,
        out_shape=jax.ShapeDtypeStruct((64, 8, 128), f32),
        in_specs=[pl.BlockSpec(memory_space=pl.ANY)],
        out_specs=pl.BlockSpec(memory_space=pl.ANY),
        scratch_shapes=[pltpu.SemaphoreType.DMA] + [pltpu.SemaphoreType.DMA((7,))] * 4,
        compiler_params=pltpu.CompilerParams(collective_id=0, has_side_effects=True),
    )(own)


def gather_kernel(own, prior, every, mine, here, s1, r1, s2, r2, s3, r3, s4, r4, sq, rq):
    x, y, z, core = place()
    row, panel = lax.axis_index("row"), lax.axis_index("panel")
    other = 1 - core

    def at(dx, dy):
        return lax.rem(x + dx, 4), lax.rem(y + dy, 4)

    def middle(i):
        cx, cy = at(core * i, other * i)
        return device(cx, cy, z, core)

    def last(i):
        cx, cy = at(other * i, core * i)
        return device(cx, cy, z, core)

    along = [device(x, y, lax.rem(z + d, 8), core) for d in range(1, 8)]
    twin = device(x, y, z, other)
    quarters = [{"row": row, "panel": lax.rem(panel + d, 4)} for d in range(1, 4)]
    far = device(x, lax.rem(y + 2, 4), z, other)
    meet(along + [middle(i) for i in range(1, 4)] + [last(i) for i in range(1, 4)] + [twin, far])

    locals_ = [
        pltpu.make_async_copy(own, every.at[panel, row], here.at[0]),
        pltpu.make_async_copy(prior.at[pl.ds(panel * 256, 256)], mine.at[panel], here.at[1]),
    ]
    for copy in locals_:
        copy.start()
    first = [send(own, every.at[panel, row], s1.at[d], r1.at[d], along[d]) for d in range(7)]
    for copy in first:
        copy.start()
    swaps = []
    for d in range(3):
        to = lax.rem(panel + d + 1, 4)
        swaps.append(send(prior.at[pl.ds(to * 256, 256)], mine.at[panel], sq.at[d], rq.at[d], quarters[d]))

    def slab(k, i):
        cx, cy = at(core * (4 - k) + other * (4 - i), core * (4 - i) + other * (4 - k))
        return every.at[cy // 2 * 2 + core, pl.ds((cx * 2 + lax.rem(cy, 2)) * 8, 8)]

    sent = list(first) + swaps

    def hand(k, i):
        copy = send(slab(k, i), slab(k, i), s4.at[k, i], r4.at[k, i], twin)
        copy.start()
        sent.append(copy)

    def onward(k):
        copies = [send(slab(k, 0), slab(k, 0), s3.at[k, i - 1], r3.at[k, i - 1], last(i)) for i in range(1, 4)]
        for copy in copies:
            copy.start()
        sent.extend(copies)
        return copies

    for copy in locals_:
        copy.wait()
    for copy in first:
        copy.wait_recv()
    second = [send(slab(0, 0), slab(0, 0), s2.at[i - 1], r2.at[i - 1], middle(i)) for i in range(1, 4)]
    for copy in second:
        copy.start()
    sent.extend(second)
    third = [onward(0)]
    hand(0, 0)
    for k in range(1, 4):
        second[k - 1].wait_recv()
        third.append(onward(k))
        hand(k, 0)
    for copy in swaps:
        copy.start()
    for k in range(4):
        for i in range(1, 4):
            third[k][i - 1].wait_recv()
            hand(k, i)
    for k in range(4):
        for i in range(4):
            send(slab(k, i), slab(k, i), s4.at[k, i], r4.at[k, i], twin).wait_recv()
    for copy in swaps:
        copy.wait_recv()
    for copy in sent:
        copy.wait_send()


def gather(own, prior):
    dma = pltpu.SemaphoreType.DMA
    width = own.shape[1]
    return pl.pallas_call(
        gather_kernel,
        out_shape=[
            jax.ShapeDtypeStruct((4, 64, 16, width), f32),
            jax.ShapeDtypeStruct((4, 256, 512), f32),
        ],
        in_specs=[pl.BlockSpec(memory_space=pl.ANY)] * 2,
        out_specs=[pl.BlockSpec(memory_space=pl.ANY)] * 2,
        scratch_shapes=[
            dma((2,)), dma((7,)), dma((7,)), dma((3,)), dma((3,)),
            dma((4, 3)), dma((4, 3)), dma((4, 4)), dma((4, 4)), dma((3,)), dma((3,)),
        ],
        compiler_params=pltpu.CompilerParams(collective_id=1, has_side_effects=True),
    )(own, prior)


def cover_kernel(er, nr, ec, nc, out):
    width = 256

    def rows(i, _):
        rs = pl.ds(pl.multiple_of(i * 8, 8), 8)
        e8, n8 = er[rs, :], nr[rs, :]
        e = [jnp.broadcast_to(e8[:, a : a + 1], (8, width)) for a in range(Q)]
        n = [jnp.broadcast_to(n8[:, a : a + 1], (8, width)) for a in range(Q)]

        def cols(j, _):
            cs = pl.ds(pl.multiple_of(j * width, width), width)
            acc = [jnp.zeros((8, width), f32) for _ in range(4)]
            for b in range(Q):
                eb = jnp.broadcast_to(ec[b : b + 1, cs], (8, width))
                nb = jnp.broadcast_to(nc[b : b + 1, cs], (8, width))
                for a in range(Q):
                    de, dn = e[a] - eb, n[a] - nb
                    acc[a % 4] = acc[a % 4] + jnp.exp2((de * de + dn * dn) * SCALE)
            out[rs, cs] = ((acc[0] + acc[1]) + (acc[2] + acc[3])) * (1.0 / (Q * Q))
            return 0

        lax.fori_loop(0, ec.shape[1] // width, cols, 0)
        return 0

    lax.fori_loop(0, er.shape[0] // 8, rows, 0)


def cover(er, nr, ec, nc):
    shape = (er.shape[0], ec.shape[1])
    return pl.pallas_call(
        cover_kernel,
        out_shape=jax.ShapeDtypeStruct(shape, f32),
        in_specs=[pl.BlockSpec(memory_space=pltpu.VMEM)] * 4,
        out_specs=pl.BlockSpec(memory_space=pltpu.VMEM),
        compiler_params=pltpu.CompilerParams(vmem_limit_bytes=VMEM_LIMIT),
    )(er, nr, ec, nc)


def split(v):
    hi = v.astype(bf16)
    return hi, (v - hi.astype(f32)).astype(bf16)


def dot3(ah, al, bh, bl):
    dot = functools.partial(lax.dot_general, dimension_numbers=NT, preferred_element_type=f32)
    return dot(ah, bh) + (dot(ah, bl) + dot(al, bh))


def factor_inverse(block):
    sub = lax.broadcasted_iota(jnp.int32, (8, 128), 0)
    lane = lax.broadcasted_iota(jnp.int32, (8, 128), 1)
    rest = [block[8 * s : 8 * s + 8, :] for s in range(16)]
    unit = [jnp.where(lane == sub + 8 * s, 1.0, 0.0).astype(f32) for s in range(16)]

    def down(v, k):
        return jnp.broadcast_to(v[k : k + 1, :], (8, 128))

    def across(v, k):
        return jnp.broadcast_to(v[:, k : k + 1], (8, 128))

    out = []
    for s in range(16):
        strip, other = rest[s], unit[s]
        cols = [across(strip, 8 * s + k) for k in range(8)]
        final = jnp.zeros((8, 128), f32)
        for k in range(8):
            pivot_row = sub == k
            pivot = down(cols[k], k)
            inverse = 1.0 / pivot
            scale = jnp.where(pivot_row, -inverse, cols[k] * inverse)

            def step(v):
                return jnp.where(pivot_row, 0.0, v) - scale * down(v, k)

            final = jnp.where(pivot_row, other * lax.rsqrt(pivot), final)
            strip, other = step(strip), step(other)
            for j in range(k + 1, 8):
                cols[j] = step(cols[j])
        out.append(final)
        for t in range(s + 1, 16):
            a, b = rest[t], unit[t]
            for k in range(8):
                c = across(rest[t], 8 * s + k)
                a = a - c * down(strip, k)
                b = b - c * down(other, k)
            rest[t], unit[t] = a, b
    return jnp.concatenate(out, axis=0)


def solve_kernel(every, mine, own_cover, out, ph, pl_, m, lh, ll, column):
    row, panel = lax.axis_index("row"), lax.axis_index("panel")
    first = (row * 4 + panel) * 4

    def halves(c, _):
        rc = pl.ds(pl.multiple_of(c * 256, 256), 256)
        for p in range(4):
            ph[p, rc, :], pl_[p, rc, :] = split(every[p, rc, 0:512])
        return 0

    lax.fori_loop(0, 4, halves, 0)
    for p in range(4):
        ph[p, 1024:1280, :], pl_[p, 1024:1280, :] = split(mine[p])
    ids = lax.broadcasted_iota(jnp.int32, (256, 256), 0)
    col = lax.broadcasted_iota(jnp.int32, (256, 256), 1)
    unit = jnp.where(ids == col, 1.0, 0.0).astype(f32)
    for j in range(4):
        cj = slice(j * 256, j * 256 + 256)
        own = jnp.where((ids < 4) & (col + j * 256 == first + ids), 1.0, 0.0).astype(f32)
        m[1024:1280, cj] = own_cover[:, cj] + own
        m[cj, cj] = every[j, cj, 512:768] + unit
        for i in range(j + 1, 4):
            ci = slice(i * 256, i * 256 + 256)
            m[ci, cj] = every[j, ci, 512:768]

    def update(j, _):
        cj = pl.ds(pl.multiple_of(j * 256, 256), 256)

        def block(i, _):
            ci = pl.ds(pl.multiple_of(i * 256, 256), 256)
            acc = m[ci, cj]
            for p in range(4):
                acc = acc - dot3(ph[p, ci, :], pl_[p, ci, :], ph[p, cj, :], pl_[p, cj, :])
            m[ci, cj] = acc
            return 0

        lax.fori_loop(j, 5, block, 0)
        return 0

    lax.fori_loop(0, 4, update, 0)

    def one(k, _):
        ck = pl.ds(pl.multiple_of(k * 128, 128), 128)

        def left(c, _):
            rc = pl.ds(pl.multiple_of(c * 256, 256), 256)

            def term(j, acc):
                cj = pl.ds(pl.multiple_of(j * 128, 128), 128)
                return acc - dot3(lh[rc, cj], ll[rc, cj], lh[ck, cj], ll[ck, cj])

            column[rc, :] = lax.fori_loop(0, k, term, m[rc, ck])
            return 0

        lax.fori_loop(k // 2, 5, left, 0)
        ih, il = split(factor_inverse(column[ck, :]))

        def right(c, _):
            rc = pl.ds(pl.multiple_of(c * 256, 256), 256)
            rh, rl = split(column[rc, :])
            v = dot3(rh, rl, ih, il)
            lh[rc, ck], ll[rc, ck] = split(v)

            @pl.when(c == 4)
            def _():
                out[:, ck] = v

            return 0

        lax.fori_loop(k // 2, 5, right, 0)
        return 0

    lax.fori_loop(0, 8, one, 0)


def solve(every, mine, own_cover):
    return pl.pallas_call(
        solve_kernel,
        out_shape=jax.ShapeDtypeStruct((256, B), f32),
        in_specs=[pl.BlockSpec(memory_space=pltpu.VMEM)] * 3,
        out_specs=pl.BlockSpec(memory_space=pltpu.VMEM),
        scratch_shapes=[
            pltpu.VMEM((4, 1280, 512), bf16), pltpu.VMEM((4, 1280, 512), bf16),
            pltpu.VMEM((1280, B), f32),
            pltpu.VMEM((1280, B), bf16), pltpu.VMEM((1280, B), bf16),
            pltpu.VMEM((1280, 128), f32),
        ],
        compiler_params=pltpu.CompilerParams(vmem_limit_bytes=VMEM_LIMIT),
    )(every, mine, own_cover)


def local(pixel_ids, quad_offsets, prior_factor):
    panel = lax.axis_index("panel")
    cell = jnp.stack([pixel_ids % 256, pixel_ids // 256])
    points = (cell[:, None, :] * 8 + quad_offsets).astype(f32)
    quarters = points.reshape(2, Q, 4, 256)[:, :, :, :4].reshape(2, Q, 16)
    packed = jnp.concatenate([quarters.reshape(4, 128), jnp.zeros((4, 128), f32)])
    got = gather_points(packed)
    cols = got[:, :4].reshape(64, 2, Q, 16).transpose(1, 2, 0, 3).reshape(2, Q, B)
    own_rows = lax.dynamic_slice_in_dim(points, panel * 256, 256, 2).transpose(0, 2, 1)
    own_cover = cover(own_rows[0], own_rows[1], cols[0], cols[1])
    some_cols = lax.dynamic_slice_in_dim(cols, panel * 256, 256, 2)
    some_rows = quarters.transpose(0, 2, 1)
    some_cover = cover(some_rows[0], some_rows[1], some_cols[0], some_cols[1])
    panel_rows = prior_factor.reshape(4, 256, 512)[:, :4].reshape(16, 512)
    every, mine = gather(jnp.concatenate([panel_rows, some_cover], axis=1), prior_factor)
    return solve(every.reshape(4, B, 768), mine, own_cover)


def solution(mesh):
    return jax.shard_map(
        local,
        mesh=mesh,
        in_specs=(P("row"), P(None, None, "row"), P("row", "panel")),
        out_specs=P(("row", "panel"), None),
        check_vma=False,
    )
```

time: 1350 us -> 284 us (0.21)
  waiting for transfers between devices: 725 us -> 0 us
  other arithmetic: 416 us -> 3.04 us
  Pallas kernels: 0 us -> 272 us
  local copies, waits for them, and re-layouts: 69 us -> 8.3 us
  matrix products: 55.5 us -> 0 us
  loops' own time: 45.8 us -> 0 us
  between operations: 19.1 us -> 0.1 us
    all_gather x2 -> x0, waiting for transfers between devices: 477 us -> none  [the longest x1 477 us: local(): lax.all_gather(schur[:per_device], ('row', 'panel'), axis=0, tiled=True)]
    pallas_call x0 -> x5, Pallas kernels: none -> 272 us  [the longest x1 91.6 us: gather(): pl.pallas_call(gather_kernel, out_shape=[jax.ShapeDtypeStruct((4, 64, 16,...]
    another operation x36 -> x0, other arithmetic: 257 us -> none  [the longest x31 173 us: local(): diag_factor = jnp.linalg.cholesky(diag_rows)]
    ppermute x63 -> x0, waiting for transfers between devices: 222 us -> none  [from_behind(): return lax.ppermute(block, axis, route)]
    reduce_sum x1024 -> x0, other arithmetic: 148 us -> none  [accumulate(): jnp.sum(jnp.exp(-(apart_east * apart_east + apart_north * apart_north) *...]
    another operation x66 -> x0, loops' own time: 45.8 us -> none  [the longest x64 42.9 us: cover_tile(): total = lax.fori_loop(0, count, accumulate, start)]
    another operation x29 -> x0, matrix products: 39.4 us -> none  [the longest x14 23.1 us: local(): diag_factor = jnp.linalg.cholesky(diag_rows)]
    another operation x98 -> x1, local copies, waits for them, and re-layouts: 26.7 us -> 0.12 us  [local(): quarters.reshape(4, 128)]
  transfers between devices with their start and end apart: 66 -> 0, of which waited for: 65 -> 0; matrix products, arithmetic and copies ran while one was open for 13% -> 0% of each run, Pallas kernels for 0% -> 0%
where the time goes in v1:
time: 284 us
  Pallas kernels  272 us (96%)
  local copies, waits for them, and re-layouts  8.3 us (3%)
  other arithmetic  3.04 us (1%)
    pallas_call x1, Pallas kernels, gather(): pl.pallas_call(gather_kernel, out_shape=[jax.ShapeDtypeStruct((4, 64, 16,...  91.6 us
    pallas_call x1, Pallas kernels, solve(): pl.pallas_call(solve_kernel, out_shape=jax.ShapeDtypeStruct((256, B), f32...  83.8 us
    pallas_call x2, Pallas kernels, cover(): pl.pallas_call(cover_kernel, out_shape=jax.ShapeDtypeStruct(shape, f32),...  79.2 us
    pallas_call x1, Pallas kernels, gather_points(): pl.pallas_call(points_kernel, out_shape=jax.ShapeDtypeStruct((64, 8, 128)...  17.7 us

profile of v1, /device:TPU:1, one launch (start us, length us, event | category | flops | bytes accessed | tf_op | source)
XLA Modules:
  0.0 283.7 jit_solution(14941178636004618550)
XLA Ops:
  0.0 0.7 add_select_fusion.1
  0.7 0.8 slice.46
  1.6 0.9 broadcast_add_fusion
  2.5 0.3 copy.9
  2.8 0.1 convert_element_type.3
  2.9 0.6 slice_bitcast_fusion.2
  3.5 0.1 copy.16
  3.7 0.1 reshape_reshape.3
  3.8 0.6 concatenate.10.own
  4.4 17.7 %shard_map.37 = f32[64,8,128]{2,1,0:T(8,128)} custom-call(f32[8,128]{1,0:T(8,128)} %concatenate.10.own), custom_call_target="tpu_custom_call" | custom-call | tf_op jit(solution)/shard_map/pallas_call | solution.py:70
  22.1 1.0 slice.39
  23.0 0.1 copy.12
  23.2 0.7 slice_bitcast_fusion
  23.9 0.2 copy.15
  24.1 0.9 squeeze.31.nc
  25.0 0.2 copy.14
  25.2 0.9 squeeze.30.ec
  26.1 76.6 %shard_map.40.own_cover = f32[256,1024]{1,0:T(8,128)} custom-call(f32[256,16]{1,0:T(8,128)} %get-tuple-element.12.er, f32[256,16]{1,0:T(8,128)} %get-tuple-element.11.nr, f32[16,1024]{1,0:T(8,128)} %squeeze.30.ec, f32[16,1024]{1,0:T(8,128)} %squeeze.31.nc), custom_call_target="tpu_custom_call" | custom-call | tf_op jit(solution)/shard_map/pallas_call | solution.py:211
  102.7 0.3 copy.13
  103.1 0.6 reshape.48
  103.7 0.6 dynamic-slice_bitcast_fusion.1
  104.3 2.7 shard_map.38
  107.0 1.3 pad_maximum_fusion.own
  108.3 91.6 %shard_map.39 = (f32[4,64,16,768]{3,2,1,0:T(8,128)}, f32[4,256,512]{2,1,0:T(8,128)}) custom-call(f32[16,768]{1,0:T(8,128)} %pad_maximum_fusion.own, f32[1024,512]{1,0:T(8,128)} %prior.1), custom_call_target="tpu_custom_call" | custom-call | tf_op jit(solution)/shard_map/pallas_call | solution.py:166
  199.9 83.8 %shard_map.41 = f32[256,1024]{1,0:T(8,128)} custom-call(f32[4,1024,768]{2,1,0:T(8,128)} %bitcast.31, f32[4,256,512]{2,1,0:T(8,128)} %get-tuple-element.8.mine, f32[256,1024]{1,0:T(8,128)} %shard_map.40.own_cover), custom_call_target="tpu_custom_call" | custom-call | tf_op jit(solution)/shard_map/pallas_call | solution.py:347
  (5 shorter events, 0.1 us)

commit v2 on v1

v2 whole, which is shorter than its diff:
```python
import functools
import math

import jax
import jax.numpy as jnp
from jax import lax
from jax.experimental import pallas as pl
from jax.experimental.pallas import tpu as pltpu
from jax.sharding import PartitionSpec as P

f32, bf16 = jnp.float32, jnp.bfloat16
MESH = pl.DeviceIdType.MESH
NT = (((1,), (1,)), ((), ()))
B = 1024
Q = 16
VMEM_LIMIT = 56 * 2**20
SCALE = -math.log2(math.e) / 64.0


def place():
    row, panel = lax.axis_index("row"), lax.axis_index("panel")
    z = lax.rem(row, 8)
    y = panel // 2 * 2 + lax.rem(row // 8, 2)
    return row // 16, y, z, lax.rem(panel, 2)


def device(x, y, z, core):
    return {"row": (x * 2 + lax.rem(y, 2)) * 8 + z, "panel": y // 2 * 2 + core}


def meet(partners):
    barrier = pltpu.get_barrier_semaphore()
    for partner in partners:
        pl.semaphore_signal(barrier, inc=1, device_id=partner, device_id_type=MESH)
    pl.semaphore_wait(barrier, len(partners))


def send(src, dst, send_sem, recv_sem, target):
    return pltpu.make_async_remote_copy(
        src_ref=src, dst_ref=dst, send_sem=send_sem, recv_sem=recv_sem,
        device_id=target, device_id_type=MESH,
    )


class Ring:
    names = ("sz", "rz", "s2", "r2", "t2", "u2", "s3", "r3", "t3", "u3", "s4", "r4")
    sizes = ((7,), (7,), (2,), (2,), (2,), (2,), (4, 2), (4, 2), (4, 2), (4, 2), (4, 4), (4, 4))

    def __init__(self, own, every, sems):
        self.own, self.every, self.sem = own, every, dict(zip(self.names, sems))
        self.x, self.y, self.z, self.core = place()
        self.row, self.panel = lax.axis_index("row"), lax.axis_index("panel")

    def slab(self, k, i, part=None):
        core, other = self.core, 1 - self.core
        cx = lax.rem(self.x + core * (4 - k) + other * (4 - i), 4)
        cy = lax.rem(self.y + core * (4 - i) + other * (4 - k), 4)
        start = (cx * 2 + lax.rem(cy, 2)) * 8
        blocks = pl.ds(start, 8) if part is None else pl.ds(start + 4 * part, 4)
        return self.every.at[cy // 2 * 2 + core, blocks]

    def neighbour(self, dim, way):
        step = 1 + 2 * way
        along_y = (1 - self.core) if dim == 0 else self.core
        cx = lax.rem(self.x + step * (1 - along_y), 4)
        cy = lax.rem(self.y + step * along_y, 4)
        return device(cx, cy, self.z, self.core)

    def z_copies(self):
        to = [device(self.x, self.y, lax.rem(self.z + d, 8), self.core) for d in range(1, 8)]
        slot = self.every.at[self.panel, self.row]
        return [send(self.own, slot, self.sem["sz"].at[d], self.sem["rz"].at[d], to[d]) for d in range(7)]

    def middle(self):
        part = self.slab(0, 0)
        return [send(part, part, self.sem["s2"].at[w], self.sem["r2"].at[w], self.neighbour(0, w)) for w in range(2)]

    def middle_far(self):
        parts = [self.slab(1, 0, 0), self.slab(3, 0, 1)]
        return [send(parts[w], parts[w], self.sem["t2"].at[w], self.sem["u2"].at[w], self.neighbour(0, w)) for w in range(2)]

    def last(self, k):
        part = self.slab(k, 0)
        return [send(part, part, self.sem["s3"].at[k, w], self.sem["r3"].at[k, w], self.neighbour(1, w)) for w in range(2)]

    def last_far(self, k):
        parts = [self.slab(k, 1, 0), self.slab(k, 3, 1)]
        return [send(parts[w], parts[w], self.sem["t3"].at[k, w], self.sem["u3"].at[k, w], self.neighbour(1, w)) for w in range(2)]

    def hand(self, k, i):
        part = self.slab(k, i)
        twin = device(self.x, self.y, self.z, 1 - self.core)
        return [send(part, part, self.sem["s4"].at[k, i], self.sem["r4"].at[k, i], twin)]

    def all(self):
        copies = self.z_copies() + self.middle() + self.middle_far()
        for k in range(4):
            copies += self.last(k) + self.last_far(k)
        return copies + [c for k in range(4) for i in range(4) for c in self.hand(k, i)]


def begin(*groups):
    for copies in groups:
        for copy in copies:
            copy.start()


def arrive(*groups):
    for copies in groups:
        for copy in copies:
            copy.wait_recv()


def cover_rows(er, nr, cols, first_tile, tiles, out, i):
    rs = pl.ds(pl.multiple_of(i * 8, 8), 8)
    e8, n8 = er[rs, :], nr[rs, :]
    e = [jnp.broadcast_to(e8[:, a : a + 1], (8, 128)) for a in range(Q)]
    n = [jnp.broadcast_to(n8[:, a : a + 1], (8, 128)) for a in range(Q)]

    def pair(j, _):
        for half in range(2):
            t = 2 * j + half
            acc = [jnp.zeros((8, 128), f32) for _ in range(4)]
            for b in range(Q):
                eb = jnp.broadcast_to(cols[first_tile + t, b : b + 1, :], (8, 128))
                nb = jnp.broadcast_to(cols[first_tile + t, Q + b : Q + b + 1, :], (8, 128))
                for a in range(Q):
                    de, dn = e[a] - eb, n[a] - nb
                    acc[a % 4] = acc[a % 4] + jnp.exp2((de * de + dn * dn) * SCALE)
            cs = pl.ds(pl.multiple_of(t * 128, 128), 128)
            out[rs, cs] = ((acc[0] + acc[1]) + (acc[2] + acc[3])) * (1.0 / (Q * Q))
        return 0

    lax.fori_loop(0, tiles // 2, pair, 0)


def gather_kernel(own, prior, pts, er, nr, se, sn, pe, ce, mine, cover, some, zpts, cols, relay, *sems):
    x, y, z, core = place()
    row, panel = lax.axis_index("row"), lax.axis_index("panel")
    count = len(Ring.names)
    here, psz, prz, ps, pr, qs, qr, qs2, qr2, ts, tr = sems[2 * count :]
    base = row // 8
    y1, ahead, back = y // 2 * 2 + 1 - lax.rem(y, 2), lax.rem(y + 1, 4), lax.rem(y + 3, 4)
    twin = device(x, y, z, 1 - core)
    along = [device(x, y, lax.rem(z + d, 8), core) for d in range(1, 8)]
    meet(
        along
        + [device(lax.rem(x + d, 4), y, z, core) for d in range(1, 4)]
        + [device(lax.rem(x + d, 4), y1, z, core) for d in range(1, 4)]
        + [device(x, ahead, z, core), device(x, back, z, core)]
        + [device(x, ahead, z, 1 - core), device(x, back, z, 1 - core), twin]
    )
    points = [send(pts, zpts.at[d], psz.at[d], prz.at[d], along[d]) for d in range(7)]
    begin(points)
    prior_ring = Ring(own, pe, sems[:count])
    cover_ring = Ring(some, ce, sems[count : 2 * count])
    local_prior = pltpu.make_async_copy(own, pe.at[panel, row], here.at[0])
    local_mine = pltpu.make_async_copy(prior.at[pl.ds(panel * 256, 256)], mine.at[panel], here.at[1])
    local_prior.start()
    local_mine.start()
    begin(prior_ring.z_copies())
    arrive(points)
    total = pts[...]
    for d in range(7):
        total = total + zpts[d]
    cols[base] = total
    spread = [
        send(cols.at[base], cols.at[base], ps.at[d], pr.at[d],
             {"row": lax.rem(base + d + 1, 8) * 8 + z, "panel": panel})
        for d in range(7)
    ]
    begin(spread)
    arrive(spread)
    for i in range(2):
        cover_rows(se, sn, cols, panel * 2, 2, some, i)
    local_cover = pltpu.make_async_copy(some, ce.at[panel, row], here.at[2])
    local_cover.start()
    begin(cover_ring.z_copies())

    def exchange():
        first, second, landing = [], [], []
        for w in range(2):
            to = (ahead, back)[w]
            source = (back, ahead)[w] // 2 * 2 + core
            for c in range(2):
                rows = (1 - y // 2) * 512 + c * 256 + w * 128
                first.append(send(prior.at[pl.ds(rows, 128)], relay.at[w, c], qs.at[w, c], qr.at[w, c],
                                  device(x, to, z, core)))
                hop = functools.partial(send, relay.at[w, c], mine.at[source, pl.ds(w * 128, 128)], qs2.at[w, c])
                second.append(hop(qr2.at[w, core], device(x, to, z, c)))
                landing.append(hop(qr2.at[w, c], device(x, to, z, c)))
        rows = (y // 2 * 2 + 1 - core) * 256
        return first, second, landing, [send(prior.at[pl.ds(rows, 256)], mine.at[panel], ts, tr, twin)]

    def start_ring(ring, local):
        local.wait()
        arrive(ring.z_copies())
        begin(ring.middle(), ring.last(0), ring.hand(0, 0))

    def middle_in(ring):
        arrive(ring.middle())
        begin(ring.middle_far(), ring.last(1), ring.last(3), ring.hand(1, 0), ring.hand(3, 0))

    def middle_far_in(ring):
        arrive(ring.middle_far())
        begin(ring.last(2), ring.hand(2, 0))

    def last_in(ring, k):
        arrive(ring.last(k))
        begin(ring.last_far(k), ring.hand(k, 1), ring.hand(k, 3))

    def last_far_in(ring):
        for k in range(4):
            arrive(ring.last_far(k))
            begin(ring.hand(k, 2))

    def at0():
        start_ring(prior_ring, local_prior)
        first, _, _, near = exchange()
        begin(first, near)

    def at1():
        middle_in(prior_ring)

    def at2():
        start_ring(cover_ring, local_cover)

    def at3():
        middle_far_in(prior_ring)
        middle_in(cover_ring)

    def at5():
        middle_far_in(cover_ring)
        first, second, _, _ = exchange()
        arrive(first)
        begin(second)

    def at8():
        last_in(prior_ring, 0)

    def at10():
        last_in(prior_ring, 1)
        last_in(prior_ring, 3)

    def at12():
        last_in(prior_ring, 2)
        last_in(cover_ring, 0)

    def at14():
        last_in(cover_ring, 1)
        last_in(cover_ring, 3)

    def at16():
        last_in(cover_ring, 2)

    def at18():
        last_far_in(prior_ring)

    def at20():
        last_far_in(cover_ring)

    steps = {0: at0, 1: at1, 2: at2, 3: at3, 5: at5, 8: at8, 10: at10, 12: at12, 14: at14, 16: at16, 18: at18, 20: at20}

    def rows(i, _):
        for when, step in steps.items():
            pl.when(i == when)(step)
        cover_rows(er, nr, cols, 0, 8, cover, i)
        return 0

    lax.fori_loop(0, 32, rows, 0)
    first, second, landing, near = exchange()
    for ring in (prior_ring, cover_ring):
        for k in range(4):
            for i in range(4):
                arrive(ring.hand(k, i))
    arrive(landing, near)
    local_mine.wait()
    for copy in points + spread + prior_ring.all() + cover_ring.all() + first + second + near:
        copy.wait_send()


def gather(own, prior, pts, er, nr, se, sn):
    dma = pltpu.SemaphoreType.DMA
    hbm, vmem = pl.BlockSpec(memory_space=pl.ANY), pl.BlockSpec(memory_space=pltpu.VMEM)
    ring = [dma(size) for size in Ring.sizes]
    return pl.pallas_call(
        gather_kernel,
        out_shape=[
            jax.ShapeDtypeStruct((4, 64, 16, 512), f32),
            jax.ShapeDtypeStruct((4, 64, 16, 256), f32),
            jax.ShapeDtypeStruct((4, 256, 512), f32),
            jax.ShapeDtypeStruct((256, B), f32),
        ],
        in_specs=[hbm, hbm, vmem, vmem, vmem, vmem, vmem],
        out_specs=[hbm, hbm, hbm, vmem],
        scratch_shapes=[
            pltpu.VMEM((16, 256), f32), pltpu.VMEM((7, 32, 128), f32), pltpu.VMEM((8, 32, 128), f32),
            pltpu.VMEM((2, 2, 128, 512), f32),
            *ring, *ring, dma((3,)), dma((7,)), dma((7,)), dma((7,)), dma((7,)),
            dma((2, 2)), dma((2, 2)), dma((2, 2)), dma((2, 2)), dma, dma,
        ],
        compiler_params=pltpu.CompilerParams(
            collective_id=0, has_side_effects=True, vmem_limit_bytes=VMEM_LIMIT
        ),
    )(own, prior, pts, er, nr, se, sn)


def split(v):
    hi = v.astype(bf16)
    return hi, (v - hi.astype(f32)).astype(bf16)


def dot3(ah, al, bh, bl):
    dot = functools.partial(lax.dot_general, dimension_numbers=NT, preferred_element_type=f32)
    return dot(ah, bh) + (dot(ah, bl) + dot(al, bh))


def factor_inverse(block):
    sub = lax.broadcasted_iota(jnp.int32, (8, 128), 0)
    lane = lax.broadcasted_iota(jnp.int32, (8, 128), 1)
    rest = [block[8 * s : 8 * s + 8, :] for s in range(16)]
    unit = [jnp.where(lane == sub + 8 * s, 1.0, 0.0).astype(f32) for s in range(16)]

    def down(v, k):
        return jnp.broadcast_to(v[k : k + 1, :], (8, 128))

    def across(v, k):
        return jnp.broadcast_to(v[:, k : k + 1], (8, 128))

    out = []
    for s in range(16):
        strip, other = rest[s], unit[s]
        cols = [across(strip, 8 * s + k) for k in range(8)]
        final = jnp.zeros((8, 128), f32)
        for k in range(8):
            pivot_row = sub == k
            pivot = down(cols[k], k)
            inverse = 1.0 / pivot
            scale = jnp.where(pivot_row, -inverse, cols[k] * inverse)

            def step(v):
                return jnp.where(pivot_row, 0.0, v) - scale * down(v, k)

            final = jnp.where(pivot_row, other * lax.rsqrt(pivot), final)
            strip, other = step(strip), step(other)
            for j in range(k + 1, 8):
                cols[j] = step(cols[j])
        out.append(final)
        for t in range(s + 1, 16):
            a, b = rest[t], unit[t]
            for k in range(8):
                c = across(rest[t], 8 * s + k)
                a = a - c * down(strip, k)
                b = b - c * down(other, k)
            rest[t], unit[t] = a, b
    return jnp.concatenate(out, axis=0)


def solve_kernel(every, panel_cover, mine, own_cover, out, ph, pl_, m, lh, ll, column):
    row, panel = lax.axis_index("row"), lax.axis_index("panel")
    first = (row * 4 + panel) * 4

    def halves(c, _):
        rc = pl.ds(pl.multiple_of(c * 256, 256), 256)
        for p in range(4):
            ph[p, rc, :], pl_[p, rc, :] = split(every[p, rc, :])
        return 0

    lax.fori_loop(0, 4, halves, 0)
    for p in range(4):
        ph[p, 1024:1280, :], pl_[p, 1024:1280, :] = split(mine[p])
    ids = lax.broadcasted_iota(jnp.int32, (256, 256), 0)
    col = lax.broadcasted_iota(jnp.int32, (256, 256), 1)
    unit = jnp.where(ids == col, 1.0, 0.0).astype(f32)
    for j in range(4):
        cj = slice(j * 256, j * 256 + 256)
        own = jnp.where((ids < 4) & (col + j * 256 == first + ids), 1.0, 0.0).astype(f32)
        m[1024:1280, cj] = own_cover[:, cj] + own
        m[cj, cj] = panel_cover[j, cj, :] + unit
        for i in range(j + 1, 4):
            ci = slice(i * 256, i * 256 + 256)
            m[ci, cj] = panel_cover[j, ci, :]

    def update(j, _):
        cj = pl.ds(pl.multiple_of(j * 256, 256), 256)

        def block(i, _):
            ci = pl.ds(pl.multiple_of(i * 256, 256), 256)
            acc = m[ci, cj]
            for p in range(4):
                acc = acc - dot3(ph[p, ci, :], pl_[p, ci, :], ph[p, cj, :], pl_[p, cj, :])
            m[ci, cj] = acc
            return 0

        lax.fori_loop(j, 5, block, 0)
        return 0

    lax.fori_loop(0, 4, update, 0)

    def one(k, _):
        ck = pl.ds(pl.multiple_of(k * 128, 128), 128)

        def left(c, _):
            rc = pl.ds(pl.multiple_of(c * 256, 256), 256)

            def term(j, acc):
                cj = pl.ds(pl.multiple_of(j * 128, 128), 128)
                return acc - dot3(lh[rc, cj], ll[rc, cj], lh[ck, cj], ll[ck, cj])

            column[rc, :] = lax.fori_loop(0, k, term, m[rc, ck])
            return 0

        lax.fori_loop(k // 2, 5, left, 0)
        ih, il = split(factor_inverse(column[ck, :]))

        def right(c, _):
            rc = pl.ds(pl.multiple_of(c * 256, 256), 256)
            rh, rl = split(column[rc, :])
            v = dot3(rh, rl, ih, il)
            lh[rc, ck], ll[rc, ck] = split(v)

            @pl.when(c == 4)
            def _():
                out[:, ck] = v

            return 0

        lax.fori_loop(k // 2, 5, right, 0)
        return 0

    lax.fori_loop(0, 8, one, 0)


def solve(every, panel_cover, mine, own_cover):
    return pl.pallas_call(
        solve_kernel,
        out_shape=jax.ShapeDtypeStruct((256, B), f32),
        in_specs=[pl.BlockSpec(memory_space=pltpu.VMEM)] * 4,
        out_specs=pl.BlockSpec(memory_space=pltpu.VMEM),
        scratch_shapes=[
            pltpu.VMEM((4, 1280, 512), bf16), pltpu.VMEM((4, 1280, 512), bf16),
            pltpu.VMEM((1280, B), f32),
            pltpu.VMEM((1280, B), bf16), pltpu.VMEM((1280, B), bf16),
            pltpu.VMEM((1280, 128), f32),
        ],
        compiler_params=pltpu.CompilerParams(vmem_limit_bytes=VMEM_LIMIT),
    )(every, panel_cover, mine, own_cover)


def local(pixel_ids, quad_offsets, prior_factor):
    row, panel = lax.axis_index("row"), lax.axis_index("panel")
    cell = jnp.stack([pixel_ids % 256, pixel_ids // 256])
    points = (cell[:, None, :] * 8 + quad_offsets).astype(f32)
    quarters = points.reshape(2, Q, 4, 256)[:, :, :, :4].reshape(2, Q, 16)
    lane = jnp.arange(128, dtype=jnp.int32) // 16
    placed = jnp.where(lane == row % 8, jnp.tile(quarters.reshape(32, 16), (1, 8)), 0.0)
    own_rows = lax.dynamic_slice_in_dim(points, panel * 256, 256, 2).transpose(0, 2, 1)
    some_rows = quarters.transpose(0, 2, 1)
    panel_rows = prior_factor.reshape(4, 256, 512)[:, :4].reshape(16, 512)
    every, panel_cover, mine, own_cover = gather(
        panel_rows, prior_factor, placed, own_rows[0], own_rows[1], some_rows[0], some_rows[1]
    )
    return solve(every.reshape(4, B, 512), panel_cover.reshape(4, B, 256), mine, own_cover)


def solution(mesh):
    return jax.shard_map(
        local,
        mesh=mesh,
        in_specs=(P("row"), P(None, None, "row"), P("row", "panel")),
        out_specs=P(("row", "panel"), None),
        check_vma=False,
    )
```

time: 284 us -> 212 us (0.75)
  the two profiles are of different devices: /device:TPU:1 before, /device:TPU:4 now
where the time goes in v2:
time: 212 us
  Pallas kernels  206 us (97%)
  local copies, waits for them, and re-layouts  3.28 us (2%)
  other arithmetic  2.33 us (1%)
    pallas_call x1, Pallas kernels, gather(): pl.pallas_call(gather_kernel, out_shape=[jax.ShapeDtypeStruct((4, 64, 16,...  122 us
    pallas_call x1, Pallas kernels, solve(): pl.pallas_call(solve_kernel, out_shape=jax.ShapeDtypeStruct((256, B), f32...  83.8 us

profile of v2, /device:TPU:4, one launch (start us, length us, event | category | flops | bytes accessed | tf_op | source)
XLA Modules:
  0.0 211.6 jit_solution(8239190531113728610)
XLA Ops:
  0.0 0.7 add_select_fusion.1
  0.7 0.8 slice.24
  1.6 0.6 reshape.41.own
  2.2 0.9 broadcast_add_fusion
  3.1 0.3 copy.7
  3.4 0.1 convert_element_type.3
  3.6 0.1 tile.10
  3.6 0.6 slice_bitcast_fusion.2
  4.2 0.1 copy.9
  4.3 0.6 broadcast_select_fusion.pts
  4.9 0.7 slice_bitcast_fusion
  5.7 122.1 %shard_map.37 = (f32[4,64,16,512]{3,2,1,0:T(8,128)}, f32[4,64,16,256]{3,2,1,0:T(8,128)}, f32[4,256,512]{2,1,0:T(8,128)}, f32[256,1024]{1,0:T(8,128)}) custom-call(f32[16,512]{1,0:T(8,128)} %reshape.41.own, f32[1024,512]{1,0:T(8,128)} %prior.1, f32[32,128]{1,0:T(8,128)} %broadcast_select_fusion.pts, f32[256,16]{1,0:T(8,128)} %get-tuple-element.14.er, ...), custom_call_target="tpu_custom_call" | custom-call | tf_op jit(solution)/shard_map/pallas_call | solution.py:286
  127.8 83.8 %shard_map.38 = f32[256,1024]{1,0:T(8,128)} custom-call(f32[4,1024,512]{2,1,0:T(8,128)} %bitcast.22, f32[4,1024,256]{2,1,0:T(8,128)} %bitcast.23, f32[4,256,512]{2,1,0:T(8,128)} %get-tuple-element.11.mine, f32[256,1024]{1,0:T(8,128)} %get-tuple-element.12.own_cover), custom_call_target="tpu_custom_call" | custom-call | tf_op jit(solution)/shard_map/pallas_call | solution.py:435
  (6 shorter events, 0.1 us)

commit v3 on v2

--- a/solution.py
+++ b/solution.py
@@ -109,6 +109,10 @@
     for copies in groups:
         for copy in copies:
             copy.wait_recv()
+
+
+def run(step):
+    step()
 
 
 def cover_rows(er, nr, cols, first_tile, tiles, out, i):
@@ -205,65 +209,45 @@
         arrive(ring.middle_far())
         begin(ring.last(2), ring.hand(2, 0))
 
-    def last_in(ring, k):
-        arrive(ring.last(k))
-        begin(ring.last_far(k), ring.hand(k, 1), ring.hand(k, 3))
+    def last_in(ring, *ks):
+        for k in ks:
+            arrive(ring.last(k))
+            begin(ring.last_far(k), ring.hand(k, 1), ring.hand(k, 3))
 
     def last_far_in(ring):
         for k in range(4):
             arrive(ring.last_far(k))
             begin(ring.hand(k, 2))
 
-    def at0():
-        start_ring(prior_ring, local_prior)
+    def exchange_out():
         first, _, _, near = exchange()
         begin(first, near)
 
-    def at1():
-        middle_in(prior_ring)
-
-    def at2():
-        start_ring(cover_ring, local_cover)
-
-    def at3():
-        middle_far_in(prior_ring)
-        middle_in(cover_ring)
-
-    def at5():
-        middle_far_in(cover_ring)
+    def exchange_on():
         first, second, _, _ = exchange()
         arrive(first)
         begin(second)
 
-    def at8():
-        last_in(prior_ring, 0)
-
-    def at10():
-        last_in(prior_ring, 1)
-        last_in(prior_ring, 3)
-
-    def at12():
-        last_in(prior_ring, 2)
-        last_in(cover_ring, 0)
-
-    def at14():
-        last_in(cover_ring, 1)
-        last_in(cover_ring, 3)
-
-    def at16():
-        last_in(cover_ring, 2)
-
-    def at18():
-        last_far_in(prior_ring)
-
-    def at20():
-        last_far_in(cover_ring)
-
-    steps = {0: at0, 1: at1, 2: at2, 3: at3, 5: at5, 8: at8, 10: at10, 12: at12, 14: at14, 16: at16, 18: at18, 20: at20}
+    steps = {
+        0: lambda: start_ring(prior_ring, local_prior),
+        2: lambda: start_ring(cover_ring, local_cover),
+        4: lambda: middle_in(prior_ring),
+        5: lambda: middle_in(cover_ring),
+        7: lambda: middle_far_in(prior_ring),
+        8: lambda: (middle_far_in(cover_ring), exchange_out()),
+        10: lambda: last_in(prior_ring, 0),
+        13: lambda: last_in(prior_ring, 1, 3),
+        15: lambda: last_in(cover_ring, 0, 1, 3),
+        18: lambda: last_in(prior_ring, 2),
+        19: lambda: last_in(cover_ring, 2),
+        20: exchange_on,
+        23: lambda: last_far_in(prior_ring),
+        25: lambda: last_far_in(cover_ring),
+    }
 
     def rows(i, _):
         for when, step in steps.items():
-            pl.when(i == when)(step)
+            pl.when(i == when)(functools.partial(run, step))
         cover_rows(er, nr, cols, 0, 8, cover, i)
         return 0
 
@@ -332,18 +316,26 @@
         strip, other = rest[s], unit[s]
         cols = [across(strip, 8 * s + k) for k in range(8)]
         final = jnp.zeros((8, 128), f32)
-        for k in range(8):
-            pivot_row = sub == k
-            pivot = down(cols[k], k)
-            inverse = 1.0 / pivot
-            scale = jnp.where(pivot_row, -inverse, cols[k] * inverse)
+        for k in range(0, 8, 2):
+            upper, lower = sub == k, sub == k + 1
+            pair = upper | lower
+            p, q, r = down(cols[k], k), down(cols[k + 1], k), down(cols[k + 1], k + 1)
+            inverse = 1.0 / (p * r - q * q)
+            ip, iq, ir = r * inverse, -(q * inverse), p * inverse
+            x, y = cols[k], cols[k + 1]
+            cx = jnp.where(upper, -ip, jnp.where(lower, -iq, x * ip + y * iq))
+            cy = jnp.where(upper, -iq, jnp.where(lower, -ir, x * iq + y * ir))
 
             def step(v):
-                return jnp.where(pivot_row, 0.0, v) - scale * down(v, k)
-
-            final = jnp.where(pivot_row, other * lax.rsqrt(pivot), final)
+                return jnp.where(pair, 0.0, v) - (cx * down(v, k) + cy * down(v, k + 1))
+
+            root = lax.rsqrt(p)
+            ox, oy = down(other, k), down(other, k + 1)
+            ratio = q * root * root
+            second = (oy - ox * ratio) * lax.rsqrt(r - q * ratio)
+            final = jnp.where(upper, ox * root, jnp.where(lower, second, final))
             strip, other = step(strip), step(other)
-            for j in range(k + 1, 8):
+            for j in range(k + 2, 8):
                 cols[j] = step(cols[j])
         out.append(final)
         for t in range(s + 1, 16):
@@ -356,19 +348,12 @@
     return jnp.concatenate(out, axis=0)
 
 
-def solve_kernel(every, panel_cover, mine, own_cover, out, ph, pl_, m, lh, ll, column):
+def solve_kernel(every, panel_cover, mine, own_cover, out, raw, ph, lo, m, lh, ll, column, sem):
     row, panel = lax.axis_index("row"), lax.axis_index("panel")
     first = (row * 4 + panel) * 4
-
-    def halves(c, _):
-        rc = pl.ds(pl.multiple_of(c * 256, 256), 256)
-        for p in range(4):
-            ph[p, rc, :], pl_[p, rc, :] = split(every[p, rc, :])
-        return 0
-
-    lax.fori_loop(0, 4, halves, 0)
-    for p in range(4):
-        ph[p, 1024:1280, :], pl_[p, 1024:1280, :] = split(mine[p])
+    loads = [pltpu.make_async_copy(every.at[p], raw.at[p], sem.at[p]) for p in range(4)]
+    for copy in loads:
+        copy.start()
     ids = lax.broadcasted_iota(jnp.int32, (256, 256), 0)
     col = lax.broadcasted_iota(jnp.int32, (256, 256), 1)
     unit = jnp.where(ids == col, 1.0, 0.0).astype(f32)
@@ -380,16 +365,26 @@
         for i in range(j + 1, 4):
             ci = slice(i * 256, i * 256 + 256)
             m[ci, cj] = panel_cover[j, ci, :]
+    for p in range(4):
+        cp = slice(p * 512, p * 512 + 512)
+        ph[1024:1280, cp], lo[1024:1280, cp] = split(mine[p])
+    for p in range(4):
+        cp = slice(p * 512, p * 512 + 512)
+        loads[p].wait()
+
+        def halves(c, _):
+            rc = pl.ds(pl.multiple_of(c * 128, 128), 128)
+            ph[rc, cp], lo[rc, cp] = split(raw[p, rc, :])
+            return 0
+
+        lax.fori_loop(0, 8, halves, 0)
 
     def update(j, _):
         cj = pl.ds(pl.multiple_of(j * 256, 256), 256)
 
         def block(i, _):
             ci = pl.ds(pl.multiple_of(i * 256, 256), 256)
-            acc = m[ci, cj]
-            for p in range(4):
-                acc = acc - dot3(ph[p, ci, :], pl_[p, ci, :], ph[p, cj, :], pl_[p, cj, :])
-            m[ci, cj] = acc
+            m[ci, cj] = m[ci, cj] - dot3(ph[ci, :], lo[ci, :], ph[cj, :], lo[cj, :])
             return 0
 
         lax.fori_loop(j, 5, block, 0)
@@ -397,51 +392,59 @@
 
     lax.fori_loop(0, 4, update, 0)
 
-    def one(k, _):
-        ck = pl.ds(pl.multiple_of(k * 128, 128), 128)
-
-        def left(c, _):
-            rc = pl.ds(pl.multiple_of(c * 256, 256), 256)
-
-            def term(j, acc):
-                cj = pl.ds(pl.multiple_of(j * 128, 128), 128)
-                return acc - dot3(lh[rc, cj], ll[rc, cj], lh[ck, cj], ll[ck, cj])
-
-            column[rc, :] = lax.fori_loop(0, k, term, m[rc, ck])
-            return 0
-
-        lax.fori_loop(k // 2, 5, left, 0)
-        ih, il = split(factor_inverse(column[ck, :]))
-
-        def right(c, _):
-            rc = pl.ds(pl.multiple_of(c * 256, 256), 256)
+    def left(k):
+        ck, before = slice(k * 128, k * 128 + 128), slice(0, k * 128)
+        for c in range(k // 2, 5):
+            rc = slice(c * 256, c * 256 + 256)
+            if k == 0:
+                column[rc, :] = m[rc, ck]
+            else:
+                column[rc, :] = m[rc, ck] - dot3(lh[rc, before], ll[rc, before], lh[ck, before], ll[ck, before])
+
+    def right(k, inverse):
+        ck = slice(k * 128, k * 128 + 128)
+        ih, il = split(inverse)
+        for c in range((k + 1) // 2, 5):
+            rc = slice(c * 256, c * 256 + 256)
             rh, rl = split(column[rc, :])
             v = dot3(rh, rl, ih, il)
-            lh[rc, ck], ll[rc, ck] = split(v)
-
-            @pl.when(c == 4)
-            def _():
+            if c < 4:
+                lh[rc, ck], ll[rc, ck] = split(v)
+            else:
+                if k < 7:
+                    lh[rc, ck], ll[rc, ck] = split(v)
                 out[:, ck] = v
 
-            return 0
-
-        lax.fori_loop(k // 2, 5, right, 0)
+    left(0)
+
+    def one(k, _):
+        inverse = factor_inverse(column[pl.ds(pl.multiple_of(k * 128, 128), 128), :])
+
+        def finish(kk):
+            right(kk, inverse)
+            if kk < 7:
+                left(kk + 1)
+
+        for kk in range(8):
+            pl.when(k == kk)(functools.partial(finish, kk))
         return 0
 
     lax.fori_loop(0, 8, one, 0)
 
 
 def solve(every, panel_cover, mine, own_cover):
+    vmem = pl.BlockSpec(memory_space=pltpu.VMEM)
     return pl.pallas_call(
         solve_kernel,
         out_shape=jax.ShapeDtypeStruct((256, B), f32),
-        in_specs=[pl.BlockSpec(memory_space=pltpu.VMEM)] * 4,
-        out_specs=pl.BlockSpec(memory_space=pltpu.VMEM),
+        in_specs=[pl.BlockSpec(memory_space=pl.ANY), vmem, vmem, vmem],
+        out_specs=vmem,
         scratch_shapes=[
-            pltpu.VMEM((4, 1280, 512), bf16), pltpu.VMEM((4, 1280, 512), bf16),
+            pltpu.VMEM((4, B, 512), f32),
+            pltpu.VMEM((1280, 2048), bf16), pltpu.VMEM((1280, 2048), bf16),
             pltpu.VMEM((1280, B), f32),
             pltpu.VMEM((1280, B), bf16), pltpu.VMEM((1280, B), bf16),
-            pltpu.VMEM((1280, 128), f32),
+            pltpu.VMEM((1280, 128), f32), pltpu.SemaphoreType.DMA((4,)),
         ],
         compiler_params=pltpu.CompilerParams(vmem_limit_bytes=VMEM_LIMIT),
     )(every, panel_cover, mine, own_cover)

time: 212 us -> 173 us (0.82)
  the two profiles are of different devices: /device:TPU:4 before, /device:TPU:1 now
where the time goes in v3:
time: 173 us; the launch traced here: 171 us
  Pallas kernels  166 us (96%)
  local copies, waits for them, and re-layouts  3.28 us (2%)
  other arithmetic  2.33 us (1%)
    pallas_call x1, Pallas kernels, gather(): pl.pallas_call(gather_kernel, out_shape=[jax.ShapeDtypeStruct((4, 64, 16,...  103 us
    pallas_call x1, Pallas kernels, solve(): pl.pallas_call(solve_kernel, out_shape=jax.ShapeDtypeStruct((256, B), f32...  62.2 us

profile of v3, /device:TPU:1, one launch (start us, length us, event | category | flops | bytes accessed | tf_op | source)
XLA Modules:
  0.0 171.4 jit_solution(13724007334417527526)
XLA Ops:
  0.0 0.7 add_select_fusion.1
  0.7 0.8 slice.24
  1.6 0.6 reshape.41.own
  2.2 0.9 broadcast_add_fusion
  3.1 0.3 copy.7
  3.4 0.1 convert_element_type.3
  3.6 0.1 tile.10
  3.6 0.6 slice_bitcast_fusion.2
  4.2 0.1 copy.9
  4.3 0.6 broadcast_select_fusion.pts
  4.9 0.7 slice_bitcast_fusion
  5.7 103.4 %shard_map.37 = (f32[4,64,16,512]{3,2,1,0:T(8,128)}, f32[4,64,16,256]{3,2,1,0:T(8,128)}, f32[4,256,512]{2,1,0:T(8,128)}, f32[256,1024]{1,0:T(8,128)}) custom-call(f32[16,512]{1,0:T(8,128)} %reshape.41.own, f32[1024,512]{1,0:T(8,128)} %prior.1, f32[32,128]{1,0:T(8,128)} %broadcast_select_fusion.pts, f32[256,16]{1,0:T(8,128)} %get-tuple-element.14.er, ...), custom_call_target="tpu_custom_call" | custom-call | tf_op jit(solution)/shard_map/pallas_call | solution.py:270
  109.0 62.2 %shard_map.38 = f32[256,1024]{1,0:T(8,128)} custom-call(f32[4,1024,512]{2,1,0:T(8,128)} %bitcast.22, f32[4,1024,256]{2,1,0:T(8,128)} %bitcast.23, f32[4,256,512]{2,1,0:T(8,128)} %get-tuple-element.11.mine, f32[256,1024]{1,0:T(8,128)} %get-tuple-element.12.own_cover), custom_call_target="tpu_custom_call" | custom-call | tf_op jit(solution)/shard_map/pallas_call | solution.py:437
  (6 shorter events, 0.1 us)

commit v4 on v3

--- a/solution.py
+++ b/solution.py
@@ -46,22 +46,23 @@
     names = ("sz", "rz", "s2", "r2", "t2", "u2", "s3", "r3", "t3", "u3", "s4", "r4")
     sizes = ((7,), (7,), (2,), (2,), (2,), (2,), (4, 2), (4, 2), (4, 2), (4, 2), (4, 4), (4, 4))
 
-    def __init__(self, own, every, sems):
+    def __init__(self, own, every, sems, turn):
         self.own, self.every, self.sem = own, every, dict(zip(self.names, sems))
         self.x, self.y, self.z, self.core = place()
+        self.turn = turn
         self.row, self.panel = lax.axis_index("row"), lax.axis_index("panel")
 
     def slab(self, k, i, part=None):
-        core, other = self.core, 1 - self.core
+        core, other = self.turn, 1 - self.turn
         cx = lax.rem(self.x + core * (4 - k) + other * (4 - i), 4)
         cy = lax.rem(self.y + core * (4 - i) + other * (4 - k), 4)
         start = (cx * 2 + lax.rem(cy, 2)) * 8
         blocks = pl.ds(start, 8) if part is None else pl.ds(start + 4 * part, 4)
-        return self.every.at[cy // 2 * 2 + core, blocks]
+        return self.every.at[cy // 2 * 2 + self.core, blocks]
 
     def neighbour(self, dim, way):
         step = 1 + 2 * way
-        along_y = (1 - self.core) if dim == 0 else self.core
+        along_y = (1 - self.turn) if dim == 0 else self.turn
         cx = lax.rem(self.x + step * (1 - along_y), 4)
         cy = lax.rem(self.y + step * along_y, 4)
         return device(cx, cy, self.z, self.core)
@@ -115,30 +116,63 @@
     step()
 
 
-def cover_rows(er, nr, cols, first_tile, tiles, out, i):
-    rs = pl.ds(pl.multiple_of(i * 8, 8), 8)
-    e8, n8 = er[rs, :], nr[rs, :]
-    e = [jnp.broadcast_to(e8[:, a : a + 1], (8, 128)) for a in range(Q)]
-    n = [jnp.broadcast_to(n8[:, a : a + 1], (8, 128)) for a in range(Q)]
-
-    def pair(j, _):
-        for half in range(2):
-            t = 2 * j + half
-            acc = [jnp.zeros((8, 128), f32) for _ in range(4)]
-            for b in range(Q):
-                eb = jnp.broadcast_to(cols[first_tile + t, b : b + 1, :], (8, 128))
-                nb = jnp.broadcast_to(cols[first_tile + t, Q + b : Q + b + 1, :], (8, 128))
-                for a in range(Q):
-                    de, dn = e[a] - eb, n[a] - nb
-                    acc[a % 4] = acc[a % 4] + jnp.exp2((de * de + dn * dn) * SCALE)
-            cs = pl.ds(pl.multiple_of(t * 128, 128), 128)
-            out[rs, cs] = ((acc[0] + acc[1]) + (acc[2] + acc[3])) * (1.0 / (Q * Q))
+TERMS = 16
+
+
+def bytes_of(v):
+    high = jnp.floor(v * (1.0 / 65536.0)) * 65536.0
+    middle = jnp.floor((v - high) * (1.0 / 256.0)) * 256.0
+    return high, middle, (v - high) - middle
+
+
+def row_terms(er, nr, lhs, tiles):
+    lane = lax.broadcasted_iota(jnp.int32, (16, 128), 1)
+
+    def tile(i, _):
+        rs = pl.ds(pl.multiple_of(i * 8, 8), 8)
+        e8, n8 = er[rs, :], nr[rs, :]
+        for a in range(0, Q, 2):
+            e, n = [
+                jnp.concatenate([jnp.broadcast_to(v[:, c : c + 1], (8, 128)) for c in (a, a + 1)]) for v in (e8, n8)
+            ]
+            eh, nh = jnp.floor(e * 0.125) * 8.0, jnp.floor(n * 0.125) * 8.0
+            high, middle, low = bytes_of(e * e + n * n)
+            terms = jnp.where(lane < 2, -2.0 * eh, jnp.where(lane < 4, -2.0 * (e - eh), -2.0 * nh))
+            terms = jnp.where((lane >= 6) & (lane < 8), -2.0 * (n - nh), terms)
+            terms = jnp.where(lane == 8, high, jnp.where(lane == 9, middle, jnp.where(lane == 10, low, terms)))
+            terms = jnp.where(lane > 10, jnp.where(lane < 14, 1.0, 0.0), terms)
+            lhs[pl.ds(pl.multiple_of(i * 128 + a * 8, 16), 16), :] = terms.astype(bf16)[:, :TERMS]
         return 0
 
-    lax.fori_loop(0, tiles // 2, pair, 0)
-
-
-def gather_kernel(own, prior, pts, er, nr, se, sn, pe, ce, mine, cover, some, zpts, cols, relay, *sems):
+    lax.fori_loop(0, tiles, tile, 0)
+
+
+def column_terms(cols, rhs, t):
+    e, n = cols[t, 0:Q, :], cols[t, Q : 2 * Q, :]
+    eh, nh = jnp.floor(e * 0.125) * 8.0, jnp.floor(n * 0.125) * 8.0
+    el, nl = e - eh, n - nh
+    one, zero = jnp.ones_like(e), jnp.zeros_like(e)
+    terms = jnp.stack([eh, el, eh, el, nh, nl, nh, nl, one, one, one, *bytes_of(e * e + n * n), zero, zero])
+    rhs[:, :, pl.ds(pl.multiple_of(t * 128, 128), 128)] = jnp.swapaxes(terms, 0, 1).astype(bf16)
+
+
+def cover_block(lhs, rhs, out, i, tiles, source, target):
+    rows = tiles * 128
+    left = lhs[pl.ds(pl.multiple_of(i * rows, rows), rows), :]
+    acc = [[jnp.zeros((8, 256), f32) for _ in range(2)] for _ in range(tiles)]
+    for b in range(Q):
+        apart = jnp.dot(left, rhs[b, :, pl.ds(pl.multiple_of(source, 256), 256)], preferred_element_type=f32)
+        near = jnp.exp2(apart * SCALE)
+        for t in range(tiles):
+            for a in range(Q):
+                r = t * 128 + a * 8
+                acc[t][a % 2] = acc[t][a % 2] + near[r : r + 8, :]
+    for t in range(tiles):
+        rs = pl.ds(pl.multiple_of(i * tiles * 8 + t * 8, 8), 8)
+        out[rs, pl.ds(pl.multiple_of(target, 256), 256)] = (acc[t][0] + acc[t][1]) * (1.0 / (Q * Q))
+
+
+def gather_kernel(own, prior, pts, er, nr, se, sn, pe, ce, mine, cover, some, zpts, cols, relay, lhs, some_lhs, rhs, *sems):
     x, y, z, core = place()
     row, panel = lax.axis_index("row"), lax.axis_index("panel")
     count = len(Ring.names)
@@ -156,13 +190,15 @@
     )
     points = [send(pts, zpts.at[d], psz.at[d], prz.at[d], along[d]) for d in range(7)]
     begin(points)
-    prior_ring = Ring(own, pe, sems[:count])
-    cover_ring = Ring(some, ce, sems[count : 2 * count])
+    prior_ring = Ring(own, pe, sems[:count], 0)
+    cover_ring = Ring(some, ce, sems[count : 2 * count], core)
     local_prior = pltpu.make_async_copy(own, pe.at[panel, row], here.at[0])
     local_mine = pltpu.make_async_copy(prior.at[pl.ds(panel * 256, 256)], mine.at[panel], here.at[1])
     local_prior.start()
     local_mine.start()
     begin(prior_ring.z_copies())
+    row_terms(se, sn, some_lhs, 2)
+    row_terms(er, nr, lhs, 32)
     arrive(points)
     total = pts[...]
     for d in range(7):
@@ -175,11 +211,18 @@
     ]
     begin(spread)
     arrive(spread)
-    for i in range(2):
-        cover_rows(se, sn, cols, panel * 2, 2, some, i)
+    for t in range(2):
+        column_terms(cols, rhs, panel * 2 + t)
+    cover_block(some_lhs, rhs, some, 0, 2, panel * 256, 0)
     local_cover = pltpu.make_async_copy(some, ce.at[panel, row], here.at[2])
     local_cover.start()
     begin(cover_ring.z_copies())
+
+    def others(t, _):
+        column_terms(cols, rhs, lax.rem(panel * 2 + t, 8))
+        return 0
+
+    lax.fori_loop(2, 8, others, 0)
 
     def exchange():
         first, second, landing = [], [], []
@@ -230,28 +273,30 @@
 
     steps = {
         0: lambda: start_ring(prior_ring, local_prior),
-        2: lambda: start_ring(cover_ring, local_cover),
-        4: lambda: middle_in(prior_ring),
-        5: lambda: middle_in(cover_ring),
-        7: lambda: middle_far_in(prior_ring),
-        8: lambda: (middle_far_in(cover_ring), exchange_out()),
-        10: lambda: last_in(prior_ring, 0),
-        13: lambda: last_in(prior_ring, 1, 3),
-        15: lambda: last_in(cover_ring, 0, 1, 3),
-        18: lambda: last_in(prior_ring, 2),
-        19: lambda: last_in(cover_ring, 2),
-        20: exchange_on,
-        23: lambda: last_far_in(prior_ring),
-        25: lambda: last_far_in(cover_ring),
+        3: lambda: start_ring(cover_ring, local_cover),
+        6: lambda: middle_in(prior_ring),
+        7: lambda: (middle_in(cover_ring), exchange_out()),
+        9: lambda: last_in(prior_ring, 0),
+        10: lambda: middle_far_in(prior_ring),
+        11: lambda: middle_far_in(cover_ring),
+        15: lambda: last_in(prior_ring, 1, 3),
+        17: lambda: last_in(cover_ring, 0),
+        18: exchange_on,
+        20: lambda: last_in(prior_ring, 2),
+        21: lambda: last_in(cover_ring, 1, 3),
+        23: lambda: last_in(cover_ring, 2),
+        27: lambda: last_far_in(prior_ring),
+        29: lambda: last_far_in(cover_ring),
     }
 
-    def rows(i, _):
+    def blocks(i, _):
         for when, step in steps.items():
             pl.when(i == when)(functools.partial(run, step))
-        cover_rows(er, nr, cols, 0, 8, cover, i)
+        at = lax.rem(i, 4) * 256
+        cover_block(lhs, rhs, cover, i // 4, 4, at, at)
         return 0
 
-    lax.fori_loop(0, 32, rows, 0)
+    lax.fori_loop(0, 32, blocks, 0)
     first, second, landing, near = exchange()
     for ring in (prior_ring, cover_ring):
         for k in range(4):
@@ -280,6 +325,7 @@
         scratch_shapes=[
             pltpu.VMEM((16, 256), f32), pltpu.VMEM((7, 32, 128), f32), pltpu.VMEM((8, 32, 128), f32),
             pltpu.VMEM((2, 2, 128, 512), f32),
+            pltpu.VMEM((4096, TERMS), bf16), pltpu.VMEM((256, TERMS), bf16), pltpu.VMEM((Q, TERMS, B), bf16),
             *ring, *ring, dma((3,)), dma((7,)), dma((7,)), dma((7,)), dma((7,)),
             dma((2, 2)), dma((2, 2)), dma((2, 2)), dma((2, 2)), dma, dma,
         ],

time: 173 us -> 147 us (0.85)
  Pallas kernels: 166 us -> 141 us
    pallas_call x1, Pallas kernels: 103 us -> 78.3 us  [gather(): pl.pallas_call(gather_kernel, out_shape=[jax.ShapeDtypeStruct((4, 64, 16,...]
where the time goes in v4:
time: 147 us; the launch traced here: 146 us
  Pallas kernels  141 us (96%)
  local copies, waits for them, and re-layouts  3.28 us (2%)
  other arithmetic  2.33 us (2%)
    pallas_call x1, Pallas kernels, gather(): pl.pallas_call(gather_kernel, out_shape=[jax.ShapeDtypeStruct((4, 64, 16,...  78.3 us
    pallas_call x1, Pallas kernels, solve(): pl.pallas_call(solve_kernel, out_shape=jax.ShapeDtypeStruct((256, B), f32...  62.2 us

profile of v4, /device:TPU:1, one launch (start us, length us, event | category | flops | bytes accessed | tf_op | source)
XLA Modules:
  0.0 146.3 jit_solution(11726189948905404328)
XLA Ops:
  0.0 0.7 add_select_fusion.1
  0.7 0.8 slice.24
  1.6 0.6 reshape.41.own
  2.2 0.9 broadcast_add_fusion
  3.1 0.3 copy.7
  3.4 0.1 convert_element_type.3
  3.6 0.1 tile.10
  3.6 0.6 slice_bitcast_fusion.2
  4.2 0.1 copy.9
  4.3 0.6 broadcast_select_fusion.pts
  4.9 0.7 slice_bitcast_fusion
  5.7 78.3 %shard_map.37 = (f32[4,64,16,512]{3,2,1,0:T(8,128)}, f32[4,64,16,256]{3,2,1,0:T(8,128)}, f32[4,256,512]{2,1,0:T(8,128)}, f32[256,1024]{1,0:T(8,128)}) custom-call(f32[16,512]{1,0:T(8,128)} %reshape.41.own, f32[1024,512]{1,0:T(8,128)} %prior.1, f32[32,128]{1,0:T(8,128)} %broadcast_select_fusion.pts, f32[256,16]{1,0:T(8,128)} %get-tuple-element.14.er, ...), custom_call_target="tpu_custom_call" | custom-call | tf_op jit(solution)/shard_map/pallas_call | solution.py:315
  84.0 62.2 %shard_map.38 = f32[256,1024]{1,0:T(8,128)} custom-call(f32[4,1024,512]{2,1,0:T(8,128)} %bitcast.22, f32[4,1024,256]{2,1,0:T(8,128)} %bitcast.23, f32[4,256,512]{2,1,0:T(8,128)} %get-tuple-element.11.mine, f32[256,1024]{1,0:T(8,128)} %get-tuple-element.12.own_cover), custom_call_target="tpu_custom_call" | custom-call | tf_op jit(solution)/shard_map/pallas_call | solution.py:483
  (6 shorter events, 0.1 us)

commit v5 on v4

--- a/solution.py
+++ b/solution.py
@@ -28,11 +28,10 @@
     return {"row": (x * 2 + lax.rem(y, 2)) * 8 + z, "panel": y // 2 * 2 + core}
 
 
-def meet(partners):
+def greet(partners):
     barrier = pltpu.get_barrier_semaphore()
     for partner in partners:
         pl.semaphore_signal(barrier, inc=1, device_id=partner, device_id_type=MESH)
-    pl.semaphore_wait(barrier, len(partners))
 
 
 def send(src, dst, send_sem, recv_sem, target):
@@ -125,15 +124,16 @@
     return high, middle, (v - high) - middle
 
 
-def row_terms(er, nr, lhs, tiles):
+def row_terms(rows, lhs, tiles):
     lane = lax.broadcasted_iota(jnp.int32, (16, 128), 1)
 
     def tile(i, _):
         rs = pl.ds(pl.multiple_of(i * 8, 8), 8)
-        e8, n8 = er[rs, :], nr[rs, :]
+        both = rows[rs, :]
         for a in range(0, Q, 2):
             e, n = [
-                jnp.concatenate([jnp.broadcast_to(v[:, c : c + 1], (8, 128)) for c in (a, a + 1)]) for v in (e8, n8)
+                jnp.concatenate([jnp.broadcast_to(both[:, c : c + 1], (8, 128)) for c in (o + a, o + a + 1)])
+                for o in (0, Q)
             ]
             eh, nh = jnp.floor(e * 0.125) * 8.0, jnp.floor(n * 0.125) * 8.0
             high, middle, low = bytes_of(e * e + n * n)
@@ -145,6 +145,31 @@
         return 0
 
     lax.fori_loop(0, tiles, tile, 0)
+
+
+def points_of(ids, offsets, lanes):
+    cell = ids[:, lanes]
+    east = (cell & 255) * 8 + offsets[0, :, lanes]
+    north = (cell >> 8) * 8 + offsets[1, :, lanes]
+    return jnp.concatenate([east, north]).astype(f32)
+
+
+def prepare(ids, offsets, pts, rows, some_rows, z, panel):
+    lane = lax.broadcasted_iota(jnp.int32, (2 * Q, 128), 1)
+    few = jnp.zeros((2 * Q, 128), f32)
+    for q in range(4):
+        quarter = points_of(ids, offsets, slice(q * 256, q * 256 + 128))
+        moved = quarter if q == 0 else pltpu.roll(quarter, 4 * q, 1)
+        few = jnp.where((lane >= 4 * q) & (lane < 4 * q + 4), moved, few)
+    again = few
+    for shift in (16, 32, 64):
+        again = again + pltpu.roll(again, shift, 1)
+    pts[...] = jnp.where(lane // 16 == z, again, 0.0)
+    blank = jnp.zeros((128 - 2 * Q, 128), f32)
+    some_rows[...] = jnp.transpose(jnp.concatenate([few, blank]))[0:16, :]
+    for h in range(2):
+        own = points_of(ids, offsets, pl.ds(pl.multiple_of(panel * 256 + h * 128, 128), 128))
+        rows[h * 128 : h * 128 + 128, :] = jnp.transpose(jnp.concatenate([own, blank]))
 
 
 def column_terms(cols, rhs, t):
@@ -172,22 +197,33 @@
         out[rs, pl.ds(pl.multiple_of(target, 256), 256)] = (acc[t][0] + acc[t][1]) * (1.0 / (Q * Q))
 
 
-def gather_kernel(own, prior, pts, er, nr, se, sn, pe, ce, mine, cover, some, zpts, cols, relay, lhs, some_lhs, rhs, *sems):
+def gather_kernel(ids, offsets, prior, pe, ce, mine, cover, pts, rows, some_rows, ends, own, some, zpts, cols, relay,
+                  lhs, some_lhs, rhs, *sems):
     x, y, z, core = place()
     row, panel = lax.axis_index("row"), lax.axis_index("panel")
     count = len(Ring.names)
-    here, psz, prz, ps, pr, qs, qr, qs2, qr2, ts, tr = sems[2 * count :]
+    quarters, here, psz, prz, ps, pr, qs, qr, qs2, qr2, ts, tr = sems[2 * count :]
     base = row // 8
     y1, ahead, back = y // 2 * 2 + 1 - lax.rem(y, 2), lax.rem(y + 1, 4), lax.rem(y + 3, 4)
     twin = device(x, y, z, 1 - core)
     along = [device(x, y, lax.rem(z + d, 8), core) for d in range(1, 8)]
-    meet(
+    greeted = (
         along
         + [device(lax.rem(x + d, 4), y, z, core) for d in range(1, 4)]
         + [device(lax.rem(x + d, 4), y1, z, core) for d in range(1, 4)]
         + [device(x, ahead, z, core), device(x, back, z, core)]
         + [device(x, ahead, z, 1 - core), device(x, back, z, 1 - core), twin]
     )
+    tops = [pltpu.make_async_copy(prior.at[pl.ds(q * 256, 8)], ends.at[q], quarters.at[q]) for q in range(4)]
+    for copy in tops:
+        copy.start()
+    greet(greeted)
+    prepare(ids, offsets, pts, rows, some_rows, z, panel)
+    for copy in tops:
+        copy.wait()
+    for h in range(2):
+        own[h * 8 : h * 8 + 8, :] = jnp.concatenate([ends[2 * h, 0:4, :], ends[2 * h + 1, 0:4, :]])
+    pl.semaphore_wait(pltpu.get_barrier_semaphore(), len(greeted))
     points = [send(pts, zpts.at[d], psz.at[d], prz.at[d], along[d]) for d in range(7)]
     begin(points)
     prior_ring = Ring(own, pe, sems[:count], 0)
@@ -197,8 +233,7 @@
     local_prior.start()
     local_mine.start()
     begin(prior_ring.z_copies())
-    row_terms(se, sn, some_lhs, 2)
-    row_terms(er, nr, lhs, 32)
+    row_terms(some_rows, some_lhs, 2)
     arrive(points)
     total = pts[...]
     for d in range(7):
@@ -210,6 +245,14 @@
         for d in range(7)
     ]
     begin(spread)
+
+    def start_ring(ring, local):
+        local.wait()
+        arrive(ring.z_copies())
+        begin(ring.middle(), ring.last(0), ring.hand(0, 0))
+
+    start_ring(prior_ring, local_prior)
+    row_terms(rows, lhs, 32)
     arrive(spread)
     for t in range(2):
         column_terms(cols, rhs, panel * 2 + t)
@@ -239,11 +282,6 @@
         rows = (y // 2 * 2 + 1 - core) * 256
         return first, second, landing, [send(prior.at[pl.ds(rows, 256)], mine.at[panel], ts, tr, twin)]
 
-    def start_ring(ring, local):
-        local.wait()
-        arrive(ring.z_copies())
-        begin(ring.middle(), ring.last(0), ring.hand(0, 0))
-
     def middle_in(ring):
         arrive(ring.middle())
         begin(ring.middle_far(), ring.last(1), ring.last(3), ring.hand(1, 0), ring.hand(3, 0))
@@ -272,21 +310,20 @@
         begin(second)
 
     steps = {
-        0: lambda: start_ring(prior_ring, local_prior),
-        3: lambda: start_ring(cover_ring, local_cover),
-        6: lambda: middle_in(prior_ring),
-        7: lambda: (middle_in(cover_ring), exchange_out()),
-        9: lambda: last_in(prior_ring, 0),
-        10: lambda: middle_far_in(prior_ring),
-        11: lambda: middle_far_in(cover_ring),
-        15: lambda: last_in(prior_ring, 1, 3),
-        17: lambda: last_in(cover_ring, 0),
-        18: exchange_on,
-        20: lambda: last_in(prior_ring, 2),
-        21: lambda: last_in(cover_ring, 1, 3),
-        23: lambda: last_in(cover_ring, 2),
-        27: lambda: last_far_in(prior_ring),
-        29: lambda: last_far_in(cover_ring),
+        0: lambda: middle_in(prior_ring),
+        1: lambda: start_ring(cover_ring, local_cover),
+        2: lambda: last_in(prior_ring, 0),
+        4: lambda: middle_far_in(prior_ring),
+        5: lambda: (middle_in(cover_ring), exchange_out()),
+        8: lambda: middle_far_in(cover_ring),
+        9: lambda: last_in(prior_ring, 1, 3),
+        13: lambda: last_in(cover_ring, 0),
+        14: lambda: last_in(prior_ring, 2),
+        15: exchange_on,
+        17: lambda: last_in(cover_ring, 1, 3),
+        20: lambda: last_in(cover_ring, 2),
+        22: lambda: last_far_in(prior_ring),
+        27: lambda: last_far_in(cover_ring),
     }
 
     def blocks(i, _):
@@ -308,7 +345,7 @@
         copy.wait_send()
 
 
-def gather(own, prior, pts, er, nr, se, sn):
+def gather(ids, offsets, prior):
     dma = pltpu.SemaphoreType.DMA
     hbm, vmem = pl.BlockSpec(memory_space=pl.ANY), pl.BlockSpec(memory_space=pltpu.VMEM)
     ring = [dma(size) for size in Ring.sizes]
@@ -320,19 +357,21 @@
             jax.ShapeDtypeStruct((4, 256, 512), f32),
             jax.ShapeDtypeStruct((256, B), f32),
         ],
-        in_specs=[hbm, hbm, vmem, vmem, vmem, vmem, vmem],
+        in_specs=[vmem, vmem, hbm],
         out_specs=[hbm, hbm, hbm, vmem],
         scratch_shapes=[
+            pltpu.VMEM((32, 128), f32), pltpu.VMEM((256, 128), f32), pltpu.VMEM((16, 128), f32),
+            pltpu.VMEM((4, 8, 512), f32), pltpu.VMEM((16, 512), f32),
             pltpu.VMEM((16, 256), f32), pltpu.VMEM((7, 32, 128), f32), pltpu.VMEM((8, 32, 128), f32),
             pltpu.VMEM((2, 2, 128, 512), f32),
             pltpu.VMEM((4096, TERMS), bf16), pltpu.VMEM((256, TERMS), bf16), pltpu.VMEM((Q, TERMS, B), bf16),
-            *ring, *ring, dma((3,)), dma((7,)), dma((7,)), dma((7,)), dma((7,)),
+            *ring, *ring, dma((4,)), dma((3,)), dma((7,)), dma((7,)), dma((7,)), dma((7,)),
             dma((2, 2)), dma((2, 2)), dma((2, 2)), dma((2, 2)), dma, dma,
         ],
         compiler_params=pltpu.CompilerParams(
             collective_id=0, has_side_effects=True, vmem_limit_bytes=VMEM_LIMIT
         ),
-    )(own, prior, pts, er, nr, se, sn)
+    )(ids, offsets, prior)
 
 
 def split(v):
@@ -394,36 +433,48 @@
     return jnp.concatenate(out, axis=0)
 
 
-def solve_kernel(every, panel_cover, mine, own_cover, out, raw, ph, lo, m, lh, ll, column, sem):
+def solve_kernel(every, panel_cover, mine, own_cover, out, raw, raw_mine, ph, lo, m, lh, ll, column, sem):
     row, panel = lax.axis_index("row"), lax.axis_index("panel")
     first = (row * 4 + panel) * 4
     loads = [pltpu.make_async_copy(every.at[p], raw.at[p], sem.at[p]) for p in range(4)]
-    for copy in loads:
+    load_mine = pltpu.make_async_copy(mine, raw_mine, sem.at[4])
+    load_own = pltpu.make_async_copy(own_cover, m.at[pl.ds(1024, 256)], sem.at[5])
+    load_cover = [
+        pltpu.make_async_copy(
+            panel_cover.at[j, pl.ds(j * 256, B - j * 256)],
+            m.at[pl.ds(j * 256, B - j * 256), pl.ds(j * 256, 256)],
+            sem.at[6 + j],
+        )
+        for j in range(4)
+    ]
+    for copy in [*loads, load_mine, load_own, *load_cover]:
         copy.start()
+    for p in range(4):
+        cp = slice(p * 512, p * 512 + 512)
+        loads[p].wait()
+
+        def halves(c, _):
+            rc = pl.ds(pl.multiple_of(c * 128, 128), 128)
+            ph[rc, cp], lo[rc, cp] = split(raw[p, rc, :])
+            return 0
+
+        lax.fori_loop(0, 8, halves, 0)
+
+    load_mine.wait()
+    for p in range(4):
+        cp = slice(p * 512, p * 512 + 512)
+        ph[1024:1280, cp], lo[1024:1280, cp] = split(raw_mine[p])
+    load_own.wait()
+    for copy in load_cover:
+        copy.wait()
     ids = lax.broadcasted_iota(jnp.int32, (256, 256), 0)
     col = lax.broadcasted_iota(jnp.int32, (256, 256), 1)
     unit = jnp.where(ids == col, 1.0, 0.0).astype(f32)
     for j in range(4):
         cj = slice(j * 256, j * 256 + 256)
         own = jnp.where((ids < 4) & (col + j * 256 == first + ids), 1.0, 0.0).astype(f32)
-        m[1024:1280, cj] = own_cover[:, cj] + own
-        m[cj, cj] = panel_cover[j, cj, :] + unit
-        for i in range(j + 1, 4):
-            ci = slice(i * 256, i * 256 + 256)
-            m[ci, cj] = panel_cover[j, ci, :]
-    for p in range(4):
-        cp = slice(p * 512, p * 512 + 512)
-        ph[1024:1280, cp], lo[1024:1280, cp] = split(mine[p])
-    for p in range(4):
-        cp = slice(p * 512, p * 512 + 512)
-        loads[p].wait()
-
-        def halves(c, _):
-            rc = pl.ds(pl.multiple_of(c * 128, 128), 128)
-            ph[rc, cp], lo[rc, cp] = split(raw[p, rc, :])
-            return 0
-
-        lax.fori_loop(0, 8, halves, 0)
+        m[1024:1280, cj] = m[1024:1280, cj] + own
+        m[cj, cj] = m[cj, cj] + unit
 
     def update(j, _):
         cj = pl.ds(pl.multiple_of(j * 256, 256), 256)
@@ -483,32 +534,21 @@
     return pl.pallas_call(
         solve_kernel,
         out_shape=jax.ShapeDtypeStruct((256, B), f32),
-        in_specs=[pl.BlockSpec(memory_space=pl.ANY), vmem, vmem, vmem],
+        in_specs=[pl.BlockSpec(memory_space=pl.ANY)] * 4,
         out_specs=vmem,
         scratch_shapes=[
-            pltpu.VMEM((4, B, 512), f32),
+            pltpu.VMEM((4, B, 512), f32), pltpu.VMEM((4, 256, 512), f32),
             pltpu.VMEM((1280, 2048), bf16), pltpu.VMEM((1280, 2048), bf16),
             pltpu.VMEM((1280, B), f32),
             pltpu.VMEM((1280, B), bf16), pltpu.VMEM((1280, B), bf16),
-            pltpu.VMEM((1280, 128), f32), pltpu.SemaphoreType.DMA((4,)),
+            pltpu.VMEM((1280, 128), f32), pltpu.SemaphoreType.DMA((10,)),
         ],
         compiler_params=pltpu.CompilerParams(vmem_limit_bytes=VMEM_LIMIT),
     )(every, panel_cover, mine, own_cover)
 
 
 def local(pixel_ids, quad_offsets, prior_factor):
-    row, panel = lax.axis_index("row"), lax.axis_index("panel")
-    cell = jnp.stack([pixel_ids % 256, pixel_ids // 256])
-    points = (cell[:, None, :] * 8 + quad_offsets).astype(f32)
-    quarters = points.reshape(2, Q, 4, 256)[:, :, :, :4].reshape(2, Q, 16)
-    lane = jnp.arange(128, dtype=jnp.int32) // 16
-    placed = jnp.where(lane == row % 8, jnp.tile(quarters.reshape(32, 16), (1, 8)), 0.0)
-    own_rows = lax.dynamic_slice_in_dim(points, panel * 256, 256, 2).transpose(0, 2, 1)
-    some_rows = quarters.transpose(0, 2, 1)
-    panel_rows = prior_factor.reshape(4, 256, 512)[:, :4].reshape(16, 512)
-    every, panel_cover, mine, own_cover = gather(
-        panel_rows, prior_factor, placed, own_rows[0], own_rows[1], some_rows[0], some_rows[1]
-    )
+    every, panel_cover, mine, own_cover = gather(pixel_ids.reshape(1, 1024), quad_offsets, prior_factor)
     return solve(every.reshape(4, B, 512), panel_cover.reshape(4, B, 256), mine, own_cover)
 
 

time: 147 us -> 152 us (1.034)
  Pallas kernels: 141 us -> 151 us
  local copies, waits for them, and re-layouts: 3.28 us -> 0 us
  other arithmetic: 2.33 us -> 0 us
    pallas_call x1, Pallas kernels: 78.3 us -> 90.9 us  [gather(): pl.pallas_call(gather_kernel, out_shape=[jax.ShapeDtypeStruct((4, 64, 16,...]
    pallas_call x1, Pallas kernels: 62.2 us -> 60.4 us  [solve(): pl.pallas_call(solve_kernel, out_shape=jax.ShapeDtypeStruct((256, B), f32...]
where the time goes in v5:
time: 152 us
  Pallas kernels  151 us (99%)
    pallas_call x1, Pallas kernels, gather(): pl.pallas_call(gather_kernel, out_shape=[jax.ShapeDtypeStruct((4, 64, 16,...  90.9 us
    pallas_call x1, Pallas kernels, solve(): pl.pallas_call(solve_kernel, out_shape=jax.ShapeDtypeStruct((256, B), f32...  60.4 us

profile of v5, /device:TPU:1, one launch (start us, length us, event | category | flops | bytes accessed | tf_op | source)
XLA Modules:
  0.0 151.5 jit_solution(16378993691804774007)
XLA Ops:
  0.0 90.9 %shard_map.37 = (f32[4,64,16,512]{3,2,1,0:T(8,128)}, f32[4,64,16,256]{3,2,1,0:T(8,128)}, f32[4,256,512]{2,1,0:T(8,128)}, f32[256,1024]{1,0:T(8,128)}) custom-call(s32[1,1024]{1,0:T(1,128)} %bitcast.5, s32[2,16,1024]{2,1,0:T(8,128)} %offsets.1, f32[1024,512]{1,0:T(8,128)} %prior.1), custom_call_target="tpu_custom_call" | custom-call | tf_op jit(solution)/shard_map/pallas_call | solution.py:352
  91.0 60.4 %shard_map.38 = f32[256,1024]{1,0:T(8,128)} custom-call(f32[4,1024,512]{2,1,0:T(8,128)} %bitcast.3, f32[4,1024,256]{2,1,0:T(8,128)} %bitcast.4, f32[4,256,512]{2,1,0:T(8,128)} %get-tuple-element.11.mine, f32[256,1024]{1,0:T(8,128)} %get-tuple-element.12.own_cover), custom_call_target="tpu_custom_call" | custom-call | tf_op jit(solution)/shard_map/pallas_call | solution.py:534

commit v6 on v5

--- a/solution.py
+++ b/solution.py
@@ -251,7 +251,6 @@
         arrive(ring.z_copies())
         begin(ring.middle(), ring.last(0), ring.hand(0, 0))
 
-    start_ring(prior_ring, local_prior)
     row_terms(rows, lhs, 32)
     arrive(spread)
     for t in range(2):
@@ -265,6 +264,7 @@
         column_terms(cols, rhs, lax.rem(panel * 2 + t, 8))
         return 0
 
+    start_ring(prior_ring, local_prior)
     lax.fori_loop(2, 8, others, 0)
 
     def exchange():
@@ -310,20 +310,20 @@
         begin(second)
 
     steps = {
-        0: lambda: middle_in(prior_ring),
-        1: lambda: start_ring(cover_ring, local_cover),
-        2: lambda: last_in(prior_ring, 0),
-        4: lambda: middle_far_in(prior_ring),
-        5: lambda: (middle_in(cover_ring), exchange_out()),
-        8: lambda: middle_far_in(cover_ring),
-        9: lambda: last_in(prior_ring, 1, 3),
-        13: lambda: last_in(cover_ring, 0),
-        14: lambda: last_in(prior_ring, 2),
-        15: exchange_on,
-        17: lambda: last_in(cover_ring, 1, 3),
-        20: lambda: last_in(cover_ring, 2),
-        22: lambda: last_far_in(prior_ring),
-        27: lambda: last_far_in(cover_ring),
+        3: lambda: start_ring(cover_ring, local_cover),
+        6: lambda: middle_in(prior_ring),
+        7: lambda: (middle_in(cover_ring), exchange_out()),
+        9: lambda: last_in(prior_ring, 0),
+        10: lambda: middle_far_in(prior_ring),
+        11: lambda: middle_far_in(cover_ring),
+        15: lambda: last_in(prior_ring, 1, 3),
+        17: lambda: last_in(cover_ring, 0),
+        18: exchange_on,
+        20: lambda: last_in(prior_ring, 2),
+        21: lambda: last_in(cover_ring, 1, 3),
+        23: lambda: last_in(cover_ring, 2),
+        27: lambda: last_far_in(prior_ring),
+        29: lambda: last_far_in(cover_ring),
     }
 
     def blocks(i, _):

time: 152 us -> 141 us (0.928)
  Pallas kernels: 151 us -> 139 us
    pallas_call x1, Pallas kernels: 90.9 us -> 79.1 us  [gather(): pl.pallas_call(gather_kernel, out_shape=[jax.ShapeDtypeStruct((4, 64, 16,...]
where the time goes in v6:
time: 141 us; the launch traced here: 140 us
  Pallas kernels  139 us (99%)
    pallas_call x1, Pallas kernels, gather(): pl.pallas_call(gather_kernel, out_shape=[jax.ShapeDtypeStruct((4, 64, 16,...  79.1 us
    pallas_call x1, Pallas kernels, solve(): pl.pallas_call(solve_kernel, out_shape=jax.ShapeDtypeStruct((256, B), f32...  60.4 us

profile of v6, /device:TPU:1, one launch (start us, length us, event | category | flops | bytes accessed | tf_op | source)
XLA Modules:
  0.0 139.6 jit_solution(10359921685605785585)
XLA Ops:
  0.0 79.1 %shard_map.37 = (f32[4,64,16,512]{3,2,1,0:T(8,128)}, f32[4,64,16,256]{3,2,1,0:T(8,128)}, f32[4,256,512]{2,1,0:T(8,128)}, f32[256,1024]{1,0:T(8,128)}) custom-call(s32[1,1024]{1,0:T(1,128)} %bitcast.5, s32[2,16,1024]{2,1,0:T(8,128)} %offsets.1, f32[1024,512]{1,0:T(8,128)} %prior.1), custom_call_target="tpu_custom_call" | custom-call | tf_op jit(solution)/shard_map/pallas_call | solution.py:352
  79.1 60.4 %shard_map.38 = f32[256,1024]{1,0:T(8,128)} custom-call(f32[4,1024,512]{2,1,0:T(8,128)} %bitcast.3, f32[4,1024,256]{2,1,0:T(8,128)} %bitcast.4, f32[4,256,512]{2,1,0:T(8,128)} %get-tuple-element.11.mine, f32[256,1024]{1,0:T(8,128)} %get-tuple-element.12.own_cover), custom_call_target="tpu_custom_call" | custom-call | tf_op jit(solution)/shard_map/pallas_call | solution.py:534
